TPU v7x, 32 devices: a whole 2x2x4 slice. The times are simulated.
32 devices in a mesh: row: 2 (over x), col: 4 (over z), fit: 4 (over y, core).
Axes of the slice: x: 2, y: 2, z: 4, core: 2. Of those that a mesh axis runs over, the one named last changes fastest.
Arguments:
- orbital_ints: bfloat16 [16, 40, 2560], P(('row', 'col'), None, 'fit'), may hold values from -0.83984375 to 0.83984375
- occ_energy: float32 [16], P(('row', 'col')), may hold values from -1.2 to -0.3
- pair_row: int32 [1024], P(('row', 'col')), may hold values from 0 to 7
- pair_col: int32 [1024], P(('row', 'col')), may hold values from 0 to 3
- virt_energy: float32 [40, 1024], P(None, ('row', 'col')), may hold values from 0.5 to 3
- amplitudes: float32 [40, 40, 1024], P(None, None, ('row', 'col')), may hold values from -1.8 to 1.8
- intersections: bfloat16 [40, 40, 16, 1024], P(None, None, 'fit', ('row', 'col')), may hold values from -1 to 1
- coupling_fock: float32 [16, 1024], P('fit', ('row', 'col')), may hold values from -0.25 to 0.25
- partner_owner: int32 [4, 1024, 4], P('fit', ('row', 'col')), may hold values from 0 to 7, all different within a row; in each aligned block of 128 rows (0 to 127, 128 to 255, ..., all dimensions but the last counted through in order) at most 128 rows name the same one
- partner_slot: int32 [4, 1024, 4], P('fit', ('row', 'col')), may hold values from 0 to 127
Outputs:
- new_amplitudes: float32 [40, 40, 1024], P(None, None, ('row', 'col'))
- residual: float32 [40, 40, 1024], P(None, None, ('row', 'col'))
Inputs may be any that keep to these rules, and one draw needn't show every extreme that they name: `partner_owner`: the 4 owners of one pair in one fit index differ; among the pairs of one group in one fit index (aligned blocks of 128 rows) no owner is named more than 128 times, a bound that some block reaches.
All inputs are finite; a program needn't handle non-finite values.
Results may differ from a plain program's by a relative error of at most 0.014.
Values may be sent and summed in bfloat16 or wider, within the bound.
A program may use at most 128 MiB of HBM per device.

v0:
```python
import math

import jax
import jax.numpy as jnp
from jax import lax
from jax.sharding import PartitionSpec as P

ITERS = 2


def on_device(
    orbital_ints,
    occ_energy,
    pair_row,
    pair_col,
    virt_energy,
    amplitudes,
    intersections,
    coupling_fock,
    partner_owner,
    partner_slot,
):
    row_count = lax.axis_size("row")
    col_count = lax.axis_size("col")
    group_count = row_count * col_count
    tile_size = amplitudes.shape[0]
    pair_count = amplitudes.shape[2]
    link_count = partner_owner.shape[2]
    capacity = 2 * pair_count * link_count // group_count
    row_ints, row_energy = (
        lax.all_gather(orbital_ints, "col", axis=0, tiled=True),
        lax.all_gather(occ_energy.astype(jnp.bfloat16), "col", axis=0, tiled=True).astype(
            occ_energy.dtype
        ),
    )
    col_ints, col_energy = (
        lax.all_gather(orbital_ints, "row", axis=0, tiled=True),
        lax.all_gather(occ_energy.astype(jnp.bfloat16), "row", axis=0, tiled=True).astype(
            occ_energy.dtype
        ),
    )
    block_width = math.gcd(pair_count, 128)
    blocks = pair_count // block_width

    def kernel_block(indices):
        first_ints = jnp.take(row_ints, indices[0], axis=0)
        second_ints = jnp.take(col_ints, indices[1], axis=0)
        return jnp.einsum(
            "pax,pbx->abp", first_ints, second_ints, preferred_element_type=jnp.float32
        )

    stacked = lax.map(
        kernel_block, (pair_row.reshape(blocks, block_width), pair_col.reshape(blocks, block_width))
    )
    partial_kernel = jnp.transpose(stacked, (1, 2, 0, 3)).reshape(tile_size, tile_size, pair_count)
    denominator = (
        virt_energy[:, None, :]
        + virt_energy[None, :, :]
        - (row_energy[pair_row] + col_energy[pair_col])[None, None, :]
    )
    owners = partner_owner[0].T.reshape(-1)
    owner_slots = partner_slot[0].T.reshape(-1)
    onehot = (owners[:, None] == jnp.arange(group_count, dtype=jnp.int32)[None, :]).astype(
        jnp.int32
    )
    position = jnp.sum((jnp.cumsum(onehot, axis=0) - 1) * onehot, axis=1)
    target = owners * capacity + position
    requests = jnp.zeros((group_count * capacity,), jnp.int32).at[target].set(owner_slots)
    incoming = lax.all_to_all(requests, ("row", "col"), split_axis=0, concat_axis=0, tiled=True)
    kernel = lax.psum(partial_kernel.astype(jnp.bfloat16), "fit").astype(jnp.float32)
    current = amplitudes
    residual = amplitudes
    for turn_index in range(ITERS):
        sent_tiles = current.astype(jnp.bfloat16)
        outgoing = jnp.take(sent_tiles, incoming, axis=2)
        returned = lax.all_to_all(outgoing, ("row", "col"), split_axis=2, concat_axis=2, tiled=True)
        coupled_tiles = jnp.take(returned, target, axis=2).reshape(
            tile_size, tile_size, link_count, pair_count
        )
        half_product = jnp.einsum(
            "abcp,bdcp->adcp", intersections, coupled_tiles, preferred_element_type=jnp.float32
        ).astype(jnp.bfloat16)
        coupled = jnp.einsum(
            "adcp,edcp->aecp", half_product, intersections, preferred_element_type=jnp.float32
        )
        coupling = jnp.sum(coupled * coupling_fock[None, None, :, :], axis=2)
        residual = (
            kernel
            + denominator * current
            - lax.psum(coupling.astype(jnp.bfloat16), "fit").astype(jnp.float32)
        )
        current = current - residual / denominator
    return (current, residual)


def solution(mesh):
    placed = (
        P(("row", "col"), None, "fit"),
        P(("row", "col")),
        P(("row", "col")),
        P(("row", "col")),
        P(None, ("row", "col")),
        P(None, None, ("row", "col")),
        P(None, None, "fit", ("row", "col")),
        P("fit", ("row", "col")),
        P("fit", ("row", "col"), None),
        P("fit", ("row", "col"), None),
    )
    return jax.shard_map(
        on_device,
        mesh=mesh,
        in_specs=placed,
        out_specs=(P(None, None, ("row", "col")), P(None, None, ("row", "col"))),
        check_vma=False,
    )
```

profile of v0, /device:TPU:1, one launch (start us, length us, event | category | flops | bytes accessed | tf_op | source)
XLA Modules:
  0.0 472.3 jit_solution(11859671098147663986)
XLA Ops:
  10.7 3.2 scatter_custom_fusion
  13.9 6.3 %all-to-all-start = ((s32[8,128,1]{1,2,0:T(1,128)}), s32[8,128,1]{1,2,0:T(1,128)S(1)}, u32[]{:S(2)}, u32[]{:S(2)}) async-start(s32[8,128,1]{1,2,0:T(1,128)} %bitcast.29), calls=%async_computation | async-start | bytes 8192 | tf_op jit(solution)/shard_map/all_to_all | solution.py:69
  22.9 2.6 all-to-all-done
  25.5 11.1 %gather_fusion.2 = bf16[1024,40,40]{2,1,0:T(8,128)(2,1)} fusion(bf16[40,40,128]{1,0,2:T(8,128)(2,1)S(1)} %copy.61, s32[1024]{0:T(1024)S(1)} %fusion.26), kind=kCustom, calls=%fused_computation.clone | custom fusion | bytes 6557696 | tf_op jit(solution)/shard_map/jit(_take)/gather | solution.py:75
  36.6 11.5 %fusion.35 = bf16[1024,40,40]{2,1,0:T(8,128)(2,1)} fusion(bf16[1024,40,40]{2,1,0:T(8,128)(2,1)} %gather_fusion.2, pred[1024]{0:T(1024)(128)(4,1)S(1)} %compare_and_fusion), kind=kLoop, calls=%fused_computation.75 | loop fusion | flops 1638400 | bytes 6554624
  48.0 17.7 %reshape.213 = bf16[8,2,102400]{2,1,0:T(2,128)(2,1)} reshape(bf16[1024,40,40]{2,1,0:T(8,128)(2,1)} %fusion.35) | data formatting | bytes 6553600
  65.8 4.6 all-to-all-start.1
  73.4 6.2 %all-reduce.1 = bf16[4]{0:T(256)(128)(2,1)S(1)} all-reduce(bf16[4]{0:T(256)(128)(2,1)S(1)} %dynamic-update-slice.1), channel_id=1, replica_groups=mesh['row'=2,'col'=4,'fit'=4] {'row'}, use_global_device_ids=true, to_apply=%add.1 | all-reduce | flops 4 | bytes 16
  79.6 49.2 %all-reduce = bf16[8]{0:T(256)(128)(2,1)S(1)} all-reduce(bf16[8]{0:T(256)(128)(2,1)S(1)} %dynamic-update-slice), channel_id=1, replica_groups=mesh['row'=2,'col'=4,'fit'=4] {'col'}, use_global_device_ids=true, to_apply=%add | all-reduce | flops 8 | bytes 32
  128.8 4.7 copy.63
  133.6 27.0 %all_gather.13 = bf16[8,40,640]{2,1,0:T(8,128)(2,1)S(1)} all-gather(bf16[2,40,640]{2,1,0:T(8,128)(2,1)S(1)} %copy-done.5), channel_id=1, replica_groups=mesh['row'=2,'col'=4,'fit'=4] {'col'}, dimensions={0}, use_global_device_ids=true | all-gather | bytes 512000 | tf_op jit(solution)/shard_map/all_gather | solution.py:31
  160.6 4.1 gather_fusion.1
  164.7 4.3 all_gather.12
  169.1 4.1 gather_fusion
  173.2 7.2 %fusion = bf16[128,40,40]{2,1,0:T(8,128)(2,1)S(1)} fusion(bf16[128,40,640]{2,1,0:T(8,128)(2,1)} %gather_fusion.1, bf16[128,40,640]{2,1,0:T(8,128)(2,1)} %gather_fusion, pred[128]{0:T(512)(128)(4,1)S(1)} %get-tuple-element.46, pred[128]{0:T(512)(128)(4,1)S(1)} %get-tuple-element.47), kind=kOutput, calls=%fused_computation.11 | convolution fusion | flops 268697600 | bytes 13517056 | tf_op jit(solution)/shard_map/while/body/eval_jaxpr/pax,pbx->abp/dot_general | solution.py:48
  180.4 1.9 copy.59
  182.3 18.7 %reshape.214 = bf16[1024,40,40]{2,1,0:T(8,128)(2,1)} reshape(bf16[8,2,102400]{2,1,0:T(2,128)(2,1)} %all-to-all-done.1) | data formatting | bytes 6553600
  201.0 7.9 %gather_fusion.3 = bf16[512,40,40]{2,1,0:T(8,128)(2,1)} fusion(bf16[40,40,1024]{1,0,2:T(8,128)(2,1)} %bitcast.87, s32[1024]{0:T(1024)S(1)} %pad_clamp_fusion), kind=kCustom, calls=%fused_computation.1.clone | custom fusion | bytes 3278848 | tf_op jit(solution)/shard_map/jit(_take)/gather | solution.py:77
  208.9 6.7 %broadcast_select_fusion.1 = bf16[512,40,40]{2,1,0:T(8,128)(2,1)} fusion(bf16[512,40,40]{2,1,0:T(8,128)(2,1)} %gather_fusion.3, pred[512]{0:T(512)(128)(4,1)S(1)} %get-tuple-element.32), kind=kLoop, calls=%fused_computation.23 | loop fusion | flops 819200 | bytes 3277312 | tf_op jit(solution)/shard_map/jit(_take)/select_n | solution.py:77
  215.6 9.7 %multiply_reduce_fusion.1 = bf16[128,40,40]{2,1,0:T(8,128)(2,1)S(1)} fusion(f32[4,128]{1,0:T(4,128)S(1)} %copy-done.10, bf16[40,40,4,128]{1,0,3,2:T(8,128)(2,1)} %copy.63, bf16[40,40,4,128]{1,0,3,2:T(8,128)(2,1)} %bitcast.89), kind=kOutput, calls=%fused_computation.10 | convolution fusion | flops 133324800 | bytes 3688448 | tf_op jit(solution)/shard_map/adcp,edcp->aecp/dot_general | solution.py:83
  228.6 7.7 %fusion.29 = f32[128]{0:T(128)S(1)} fusion(f32[]{:T(128)} %bitcast.11, f32[]{:T(128)} %bitcast.12, f32[]{:T(128)} %bitcast.13, f32[]{:T(128)} %bitcast.14, f32[]{:T(128)} %bitcast.2, f32[]{:T(128)} %bitcast.3, f32[]{:T(128)} %bitcast.4, f32[]{:T(128)} %bitcast.5, f32[]{:T(128)} %bitcast.6, f32[]{:T(128)} %bitcast.7, f32[]{:T(128)} %bitcast.8, f32[]{:T(128)} %bitcast.9, ...), kind=kLoop, calls=%fused_computation.70 | loop fusion | flops 3456 | bytes 1584 | tf_op jit(solution)/shard_map/add | solution.py:59
  236.4 30.7 %all-reduce.8.cloned.1.call-done = (bf16[40,40,128]{2,1,0:T(8,128)(2,1)}, bf16[40,40,128]{2,1,0:T(8,128)(2,1)}) async-done(((bf16[40,40,128]{2,1,0:T(8,128)(2,1)}, bf16[40,40,128]{2,1,0:T(8,128)(2,1)}), (bf16[40,40,128]{2,1,0:T(8,128)(2,1)}, bf16[40,40,128]{2,1,0:T(8,128)(2,1)})) %all-reduce.8.cloned.1.call-update) | async-done | bytes 819216 | tf_op jit(solution)/shard_map/psum | solution.py:70
  269.9 11.1 %gather_fusion.4 = bf16[1024,40,40]{2,1,0:T(8,128)(2,1)} fusion(bf16[40,40,128]{1,0,2:T(8,128)(2,1)S(1)} %copy.67, s32[1024]{0:T(1024)S(1)} %fusion.26), kind=kCustom, calls=%fused_computation.2.clone | custom fusion | bytes 6557696 | tf_op jit(solution)/shard_map/jit(_take)/gather | solution.py:75
  281.0 11.5 %fusion.36 = bf16[1024,40,40]{2,1,0:T(8,128)(2,1)} fusion(bf16[1024,40,40]{2,1,0:T(8,128)(2,1)} %gather_fusion.4, pred[1024]{0:T(1024)(128)(4,1)S(1)} %compare_and_fusion), kind=kLoop, calls=%fused_computation.76 | loop fusion | flops 1638400 | bytes 6554624
  292.5 16.9 %reshape.215 = bf16[8,2,102400]{2,1,0:T(2,128)(2,1)S(1)} reshape(bf16[1024,40,40]{2,1,0:T(8,128)(2,1)} %fusion.36) | data formatting | bytes 6553600
  309.4 78.5 %all_to_all.22 = bf16[8,2,102400]{2,1,0:T(2,128)(2,1)} all-to-all(bf16[8,2,102400]{2,1,0:T(2,128)(2,1)S(1)} %reshape.215), channel_id=1, replica_groups=mesh['row'=2,'col'=4,'fit'=4] {'row','col'}, dimensions={0} | all-to-all | bytes 6553600 | tf_op jit(solution)/shard_map/all_to_all | solution.py:76
  387.9 18.7 %reshape.216 = bf16[1024,40,40]{2,1,0:T(8,128)(2,1)} reshape(bf16[8,2,102400]{2,1,0:T(2,128)(2,1)} %all_to_all.22) | data formatting | bytes 6553600
  406.6 7.9 %gather_fusion.5 = bf16[512,40,40]{2,1,0:T(8,128)(2,1)} fusion(bf16[40,40,1024]{1,0,2:T(8,128)(2,1)} %bitcast.86, s32[1024]{0:T(1024)S(1)} %pad_clamp_fusion), kind=kCustom, calls=%fused_computation.3.clone | custom fusion | bytes 3278848 | tf_op jit(solution)/shard_map/jit(_take)/gather | solution.py:77
  414.5 6.7 %broadcast_select_fusion = bf16[512,40,40]{2,1,0:T(8,128)(2,1)} fusion(bf16[512,40,40]{2,1,0:T(8,128)(2,1)} %gather_fusion.5, pred[512]{0:T(512)(128)(4,1)S(1)} %get-tuple-element.32), kind=kLoop, calls=%fused_computation.22 | loop fusion | flops 819200 | bytes 3277312 | tf_op jit(solution)/shard_map/jit(_take)/select_n | solution.py:77
  421.1 9.7 %multiply_reduce_fusion = bf16[128,40,40]{2,1,0:T(8,128)(2,1)S(1)} fusion(f32[4,128]{1,0:T(4,128)S(1)} %copy-done.10, bf16[40,40,4,128]{1,0,3,2:T(8,128)(2,1)} %copy.63, bf16[40,40,4,128]{1,0,3,2:T(8,128)(2,1)} %bitcast.88), kind=kOutput, calls=%fused_computation.9 | convolution fusion | flops 133324800 | bytes 3688448 | tf_op jit(solution)/shard_map/adcp,edcp->aecp/dot_general | solution.py:83
  432.6 30.3 %all-reduce.6.cloned.1.call-done = bf16[40,40,128]{2,1,0:T(8,128)(2,1)} async-done(((bf16[40,40,128]{2,1,0:T(8,128)(2,1)}), bf16[40,40,128]{2,1,0:T(8,128)(2,1)}) %all-reduce.6.cloned.1.call-update) | async-done | bytes 409616 | tf_op jit(solution)/shard_map/psum | solution.py:90
  462.8 2.6 divide_subtract_fusion
  (65 shorter events, 16.0 us)
Async XLA Ops:
  13.9 11.6 %all-to-all-start = ((s32[8,128,1]{1,2,0:T(1,128)}), s32[8,128,1]{1,2,0:T(1,128)S(1)}, u32[]{:S(2)}, u32[]{:S(2)}) async-start(s32[8,128,1]{1,2,0:T(1,128)} %bitcast.29), calls=%async_computation | async-start | bytes 8192 | tf_op jit(solution)/shard_map/all_to_all | solution.py:69
  65.7 4.7 copy-start.13
  65.7 5.3 %copy-start.12 = (u32[32]{0:T(128)S(1)}, u32[32]{0:T(128)}, u32[]{:S(2)}) copy-start(u32[32]{0:T(128)} %constant.103) | copy-start | bytes 388
  65.7 7.2 %copy-start.11 = (f32[2]{0:T(128)S(1)}, f32[2]{0:T(128)}, u32[]{:S(2)}) copy-start(f32[2]{0:T(128)} %param.15) | copy-start | bytes 28
  65.7 63.1 %copy-start.2 = (bf16[40,40,4,128]{3,2,1,0:T(4,128)(2,1)S(1)}, bf16[40,40,4,128]{3,2,1,0:T(4,128)(2,1)}, u32[]{:S(2)}) copy-start(bf16[40,40,4,128]{3,2,1,0:T(4,128)(2,1)} %param.20) | copy-start | bytes 4915204
  65.7 67.8 %copy-start.9 = (s32[128]{0:T(128)S(1)}, s32[128]{0:T(128)}, u32[]{:S(2)}) copy-start(s32[128]{0:T(128)} %param.16) | copy-start | bytes 1540
  65.8 67.8 %copy-start.5 = (bf16[2,40,640]{2,1,0:T(8,128)(2,1)S(1)}, bf16[2,40,640]{2,1,0:T(8,128)(2,1)}, u32[]{:S(2)}) copy-start(bf16[2,40,640]{2,1,0:T(8,128)(2,1)} %param.14) | copy-start | bytes 307204
  65.8 116.6 %all-to-all-start.1 = ((bf16[8,2,102400]{2,1,0:T(2,128)(2,1)}), bf16[8,2,102400]{2,1,0:T(2,128)(2,1)}, u32[]{:S(2)}, u32[]{:S(2)}) async-start(bf16[8,2,102400]{2,1,0:T(2,128)(2,1)} %reshape.213), calls=%async_computation.1 | async-start | bytes 6553600 | tf_op jit(solution)/shard_map/all_to_all | solution.py:76
  70.4 196.7 %all-reduce.8.cloned.1.call-start = ((), (), s32[]{:S(2)}) async-start(), calls=%async_computation.4 | async-start | bytes 1638400 | tf_op jit(solution)/shard_map/psum | solution.py:70
  160.6 8.5 %copy-start.8 = (s32[128]{0:T(128)S(1)}, s32[128]{0:T(128)}, u32[]{:S(2)}) copy-start(s32[128]{0:T(128)} %param.17) | copy-start | bytes 1540
  173.2 9.1 %copy-start.7 = (s32[1,128,4]{1,2,0:T(4,128)S(1)}, s32[1,128,4]{1,2,0:T(4,128)}, u32[]{:S(2)}) copy-start(s32[1,128,4]{1,2,0:T(4,128)} %param.22) | copy-start | bytes 6148
  208.9 6.7 %copy-start.10 = (f32[4,128]{1,0:T(4,128)S(1)}, f32[4,128]{1,0:T(4,128)}, u32[]{:S(2)}) copy-start(f32[4,128]{1,0:T(4,128)} %param.21) | copy-start | bytes 6148
  215.6 51.5 %copy-start = (f32[40,40,128]{2,1,0:T(8,128)S(1)}, f32[40,40,128]{2,1,0:T(8,128)}, u32[]{:S(2)}) copy-start(f32[40,40,128]{2,1,0:T(8,128)} %param.19) | copy-start | bytes 2457604
  215.6 51.5 %copy-start.6 = (f32[40,128]{1,0:T(8,128)S(1)}, f32[40,128]{1,0:T(8,128)}, u32[]{:S(2)}) copy-start(f32[40,128]{1,0:T(8,128)} %param.18) | copy-start | bytes 61444
  227.0 235.8 %all-reduce.6.cloned.1.call-start = ((), (), s32[]{:S(2)}) async-start(), calls=%async_computation.3 | async-start | bytes 819200 | tf_op jit(solution)/shard_map/psum | solution.py:90
  421.1 41.7 %copy-start.1 = (f32[40,40,128]{2,1,0:T(8,128)S(1)}, f32[40,40,128]{2,1,0:T(8,128)}, u32[]{:S(2)}) copy-start(f32[40,40,128]{2,1,0:T(8,128)} %param.19) | copy-start | bytes 2457604
  421.1 41.7 %copy-start.3 = (bf16[40,40,128]{2,1,0:T(8,128)(2,1)S(1)}, bf16[40,40,128]{2,1,0:T(8,128)(2,1)}, u32[]{:S(2)}) copy-start(bf16[40,40,128]{2,1,0:T(8,128)(2,1)} %get-tuple-element.28) | copy-start | bytes 1228804
  421.1 41.7 %copy-start.4 = (bf16[40,40,128]{2,1,0:T(8,128)(2,1)S(1)}, bf16[40,40,128]{2,1,0:T(8,128)(2,1)}, u32[]{:S(2)}) copy-start(bf16[40,40,128]{2,1,0:T(8,128)(2,1)} %get-tuple-element.29) | copy-start | bytes 1228804
Sparse Core Ops, SparseCore 0:
  227.1 39.8 all-reduce.7
  432.7 30.0 all-reduce.5
where the time goes:
time: 475 us; the launch traced here: 472 us
  blocking collectives  165 us (35%)
  local copies, waits for them, and re-layouts  138 us (29%)
  waiting for transfers between devices  63.5 us (13%)
  other arithmetic  52.6 us (11%)
  matrix products  26.6 us (6%)
  between operations  15.5 us (3%)
  starting transfers between devices  11.2 us (2%)
    all_to_all x1, blocking collectives, on_device(): lax.all_to_all(outgoing, ('row', 'col'), split_axis=2, concat_axis=2, til...  78.5 us
    unnamed x39, local copies, waits for them, and re-layouts  78.5 us
    unnamed x2, blocking collectives  55.4 us
    psum x1, waiting for transfers between devices, on_device(): lax.psum(partial_kernel.astype(jnp.bfloat16), 'fit').astype(jnp.float32)  30.7 us
    psum x1, waiting for transfers between devices, on_device(): lax.psum(coupling.astype(jnp.bfloat16), 'fit').astype(jnp.float32)  30.3 us
    all_gather x1, blocking collectives, on_device(): lax.all_gather(orbital_ints, 'col', axis=0, tiled=True)  27 us
    unnamed x2, other arithmetic  22.9 us
    gather x2, local copies, waits for them, and re-layouts, on_device(): outgoing = jnp.take(sent_tiles, incoming, axis=2)  22.1 us
  transfers between devices with their start and end apart: 4, of which 3 were waited for; matrix products, arithmetic and copies ran while one was open for 8% of the time, Pallas kernels for 0%

commit v1 on v0

v1 whole, which is shorter than its diff:
```python
import functools

import jax
import jax.numpy as jnp
from jax import lax
from jax.experimental import pallas as pl
from jax.experimental.pallas import tpu as pltpu
from jax.sharding import PartitionSpec as P

ITERS = 2
LANES = 128
MESH = pl.DeviceIdType.MESH
ANY = pl.BlockSpec(memory_space=pl.ANY)
VMEM_LIMIT = 60 * 1024 * 1024


class Sender:
    def __init__(self, send_sems):
        self.send_sems, self.started = send_sems, []

    def send(self, source, target, recv_sem, device, when=None):
        copy = pltpu.make_async_remote_copy(
            src_ref=source,
            dst_ref=target,
            send_sem=self.send_sems.at[len(self.started)],
            recv_sem=recv_sem,
            device_id=device,
            device_id_type=MESH,
        )
        self.started.append((copy, when))
        guarded(when, copy.start)

    def finish(self):
        for copy, when in self.started:
            guarded(when, copy.wait_send)


def guarded(when, action):
    if when is None:
        action()
    else:
        pl.when(when)(action)


def both(first, second):
    return second if first is None else first if second is None else jnp.logical_and(first, second)


def greet(axes):
    barrier = pltpu.get_barrier_semaphore()
    total = 0
    for axis in axes:
        count = lax.axis_size(axis)
        here = lax.axis_index(axis)
        for step in range(1, count):
            pl.semaphore_signal(
                barrier, inc=1, device_id={axis: lax.rem(here + step, count)}, device_id_type=MESH
            )
            total += 1
    pl.semaphore_wait(barrier, total)


def gather_kernel(sizes, with_ints, *refs):
    if with_ints:
        own, ints, energy, tiles, row_ints, col_ints, row_en, col_en = refs[:8]
        send_sems, recv_sems, part_sems, int_sems, local_sems = refs[8:]
    else:
        own, tiles, send_sems, recv_sems, part_sems, local_sems = refs
    R, C = lax.axis_size("row"), lax.axis_size("col")
    r, c, f = lax.axis_index("row"), lax.axis_index("col"), lax.axis_index("fit")
    partner = {"fit": f + 1 - 2 * lax.rem(f, 2)}
    half = sum(sizes)
    mine = lax.rem(f, 2) * half
    theirs = half - mine
    me = r * C + c
    greet(("row", "col", "fit"))
    out = Sender(send_sems)
    offsets = (0, sizes[0])

    def place(piece, group, base=mine):
        return tiles.at[group, pl.ds(base + offsets[piece], sizes[piece])]

    def await_copy(piece, group, sem, base=mine, when=None):
        ref = place(piece, group, base)
        copy = pltpu.make_async_remote_copy(
            src_ref=ref, dst_ref=ref, send_sem=send_sems.at[0], recv_sem=sem,
            device_id=partner, device_id_type=MESH,
        )
        guarded(when, copy.wait_recv)

    def along(piece, group, step, when=None, source=None):
        inside = c + 1 < C if step > 0 else c > 0
        out.send(
            place(piece, group) if source is None else source, place(piece, group),
            recv_sems.at[piece, group], {"col": c + step}, both(when, inside),
        )

    def across(piece, group, when=None, source=None):
        for step in range(1, R):
            out.send(
                place(piece, group) if source is None else source, place(piece, group),
                recv_sems.at[piece, group], {"row": lax.rem(r + step, R)}, when,
            )

    def beside(piece, group, when=None):
        out.send(place(piece, group), place(piece, group), part_sems.at[piece, group], partner, when)

    def own_piece(piece):
        return own.at[pl.ds(mine + offsets[piece], sizes[piece])]

    across(1, me, source=own_piece(1))
    for step in (1, -1):
        along(0, me, step, source=own_piece(0))
    if with_ints:
        def int_wait(target, sem, when=None):
            copy = pltpu.make_async_remote_copy(
                src_ref=target, dst_ref=target, send_sem=send_sems.at[0], recv_sem=sem,
                device_id=partner, device_id_type=MESH,
            )
            guarded(when, copy.wait_recv)

        for step in (1, -1):
            inside = c + 1 < C if step > 0 else c > 0
            out.send(ints, row_ints.at[c], int_sems.at[0, c], {"col": c + step}, inside)
        for step in range(1, R):
            to = {"row": lax.rem(r + step, R)}
            out.send(ints, col_ints.at[r], int_sems.at[1, r], to)
            out.send(energy, col_en.at[r], int_sems.at[3, r], to)
        for step in range(1, C):
            to = {"col": lax.rem(c + step, C)}
            out.send(energy, row_en.at[c], int_sems.at[2, c], to)
    for step in (1, -1):
        along(1, me, step, source=own_piece(1))
    across(0, me, source=own_piece(0))
    local = [pltpu.make_async_copy(own, tiles.at[me], local_sems.at[0])]
    if with_ints:
        local += [
            pltpu.make_async_copy(ints, row_ints.at[c], local_sems.at[1]),
            pltpu.make_async_copy(ints, col_ints.at[r], local_sems.at[2]),
            pltpu.make_async_copy(energy, row_en.at[c], local_sems.at[3]),
            pltpu.make_async_copy(energy, col_en.at[r], local_sems.at[4]),
        ]
    for copy in local:
        copy.start()
    for other in range(1, R):
        group = lax.rem(r + other, R) * C + c
        await_copy(1, group, recv_sems.at[1, group])
        for step in (1, -1):
            along(1, group, step)
        beside(1, group)
    for distance in range(1, C):
        for step in (1, -1):
            source = c - step * distance
            there = jnp.logical_and(source >= 0, source < C)
            column = jnp.clip(source, 0, C - 1)
            group = r * C + column
            await_copy(0, group, recv_sems.at[0, group], when=there)
            if distance < C - 1:
                along(0, group, step, there)
            across(0, group, there)
            beside(0, group, there)
            for other in range(R):
                group = lax.rem(r + other, R) * C + column
                await_copy(1, group, recv_sems.at[1, group], when=there)
                if distance < C - 1:
                    along(1, group, step, there)
                beside(1, group, there)
            if with_ints:
                int_wait(row_ints.at[column], int_sems.at[0, column], there)
                if distance < C - 1:
                    inside = c + 1 < C if step > 0 else c > 0
                    out.send(
                        row_ints.at[column], row_ints.at[column], int_sems.at[0, column],
                        {"col": c + step}, both(there, inside),
                    )
    for other in range(1, R):
        for turn in range(C):
            group = lax.rem(r + other, R) * C + lax.rem(c + turn, C)
            await_copy(0, group, recv_sems.at[0, group])
            beside(0, group)
    if with_ints:
        for step in range(1, R):
            row = lax.rem(r + step, R)
            int_wait(col_ints.at[row], int_sems.at[1, row])
            int_wait(col_en.at[row], int_sems.at[3, row])
        for step in range(1, C):
            column = lax.rem(c + step, C)
            int_wait(row_en.at[column], int_sems.at[2, column])
    for step in range(1, R * C):
        group = lax.rem(me + step, R * C)
        for piece in range(2):
            await_copy(piece, group, part_sems.at[piece, group], base=theirs)
    for copy in local:
        copy.wait()
    out.finish()


def gather(packed, collective_id, ints=None, energy=None):
    R, C = lax.axis_size("row"), lax.axis_size("col")
    G = R * C
    with_ints = ints is not None
    half = packed.shape[0] // 2
    first = (half * 3 + 4) // 5
    shapes = [jax.ShapeDtypeStruct((G,) + packed.shape, packed.dtype)]
    operands = [packed]
    if with_ints:
        operands += [ints, energy]
        shapes += [
            jax.ShapeDtypeStruct((C,) + ints.shape, ints.dtype),
            jax.ShapeDtypeStruct((R,) + ints.shape, ints.dtype),
            jax.ShapeDtypeStruct((C,) + energy.shape, energy.dtype),
            jax.ShapeDtypeStruct((R,) + energy.shape, energy.dtype),
        ]
    scratch = [
        pltpu.SemaphoreType.DMA((16 * R * C + 32,)),
        pltpu.SemaphoreType.DMA((2, G)),
        pltpu.SemaphoreType.DMA((2, G)),
    ]
    if with_ints:
        scratch.append(pltpu.SemaphoreType.DMA((4, max(R, C))))
    scratch.append(pltpu.SemaphoreType.DMA((5,)))
    return pl.pallas_call(
        functools.partial(gather_kernel, (first, half - first), with_ints),
        out_shape=shapes,
        in_specs=[ANY] * len(operands),
        out_specs=[ANY] * len(shapes),
        scratch_shapes=scratch,
        name="gather_ints" if with_ints else "gather_tiles",
        compiler_params=pltpu.CompilerParams(
            collective_id=collective_id, has_side_effects=True, vmem_limit_bytes=VMEM_LIMIT
        ),
    )(*operands)


def sum_kernel(part, total, inbox, result, send_sems, recv_sems, gather_sems, local_sem):
    F = lax.axis_size("fit")
    f = lax.axis_index("fit")
    rows = part.shape[0] // F
    greet(("fit",))
    out = Sender(send_sems)
    for step in range(1, F):
        to = lax.rem(f + step, F)
        out.send(
            part.at[pl.ds(to * rows, rows)], inbox.at[step - 1], recv_sems.at[step - 1], {"fit": to}
        )
    value = part[pl.ds(f * rows, rows)].astype(jnp.float32)
    for step in range(1, F):
        pltpu.make_async_remote_copy(
            src_ref=inbox.at[step - 1], dst_ref=inbox.at[step - 1], send_sem=send_sems.at[0],
            recv_sem=recv_sems.at[step - 1], device_id={"fit": lax.rem(f + step, F)},
            device_id_type=MESH,
        ).wait_recv()
        value = value + inbox[step - 1].astype(jnp.float32)
    result[...] = value.astype(result.dtype)
    target = total.at[pl.ds(f * rows, rows)]
    for step in range(1, F):
        out.send(result, target, gather_sems.at[step - 1], {"fit": lax.rem(f + step, F)})
    local = pltpu.make_async_copy(result, target, local_sem)
    local.start()
    for step in range(1, F):
        source = lax.rem(f + F - step, F)
        ref = total.at[pl.ds(source * rows, rows)]
        pltpu.make_async_remote_copy(
            src_ref=ref, dst_ref=ref, send_sem=send_sems.at[0], recv_sem=gather_sems.at[step - 1],
            device_id={"fit": source}, device_id_type=MESH,
        ).wait_recv()
    local.wait()
    out.finish()


def fit_sum(part, collective_id):
    F = lax.axis_size("fit")
    piece = (part.shape[0] // F,) + part.shape[1:]
    return pl.pallas_call(
        sum_kernel,
        out_shape=jax.ShapeDtypeStruct(part.shape, part.dtype),
        in_specs=[pl.BlockSpec(memory_space=pltpu.VMEM)],
        out_specs=ANY,
        scratch_shapes=[
            pltpu.VMEM((F - 1,) + piece, part.dtype),
            pltpu.VMEM(piece, part.dtype),
            pltpu.SemaphoreType.DMA((2 * F,)),
            pltpu.SemaphoreType.DMA((F,)),
            pltpu.SemaphoreType.DMA((F,)),
            pltpu.SemaphoreType.DMA,
        ],
        name="fit_sum",
        compiler_params=pltpu.CompilerParams(collective_id=collective_id, has_side_effects=True),
    )(part)


def couple_kernel(block, pair_count, first_turn, row_ref, shift_ref, fock_ref, pick_ref, tiles, inter, base, out, *kept):
    links, size = inter.shape[1], inter.shape[2]
    lane = lax.broadcasted_iota(jnp.int32, (1, LANES), 1)
    first = pl.program_id(0) * block

    def pair(q, carry):
        p = first + q
        halves, sides = [], []
        for k in range(links):
            n = k * pair_count + p
            side = inter[q, k]
            half = jnp.dot(side[:, :size], tiles[row_ref[n]], preferred_element_type=jnp.float32)
            shift = shift_ref[n]
            chosen = jnp.logical_and(lane >= shift, lane < shift + size)
            halves.append((half * jnp.where(chosen, fock_ref[n], 0.0)).astype(jnp.bfloat16))
            sides.append(side)
        coupling = lax.dot_general(
            jnp.concatenate(halves, axis=1), jnp.concatenate(sides, axis=1),
            (((1,), (1,)), ((), ())), preferred_element_type=jnp.float32,
        )
        if first_turn:
            kept[0][q] = coupling
            out[q] = (base[pick_ref[p]] - coupling).astype(out.dtype)
        else:
            out[q] = (base[q] - coupling).astype(out.dtype)
        return carry

    lax.fori_loop(0, block, pair, 0, unroll=4)


def couple(first_turn, rows, shifts, fock, picks, tiles, inter, base):
    pair_count, links, size, _ = inter.shape
    block = 16
    smem = pl.BlockSpec(memory_space=pltpu.SMEM)
    whole = lambda shape: pl.BlockSpec(shape, lambda i: (0, 0, 0), pipeline_mode=pl.Buffered(1))
    by_pair = pl.BlockSpec((block, size, size), lambda i: (i, 0, 0))
    shapes = [jax.ShapeDtypeStruct((pair_count, size, size), jnp.bfloat16)]
    if first_turn:
        shapes.append(jax.ShapeDtypeStruct((pair_count, size, size), jnp.float32))
    return pl.pallas_call(
        functools.partial(couple_kernel, block, pair_count, first_turn),
        grid=(pair_count // block,),
        out_shape=shapes,
        in_specs=[
            smem, smem, smem, smem,
            whole(tiles.shape),
            pl.BlockSpec((block, links, size, LANES), lambda i: (i, 0, 0, 0)),
            whole(base.shape) if first_turn else by_pair,
        ],
        out_specs=[by_pair] * len(shapes),
        name="couple",
        compiler_params=pltpu.CompilerParams(vmem_limit_bytes=VMEM_LIMIT),
    )(rows, shifts, fock, picks, tiles, inter, base)


def on_device(
    orbital_ints,
    occ_energy,
    pair_row,
    pair_col,
    virt_energy,
    amplitudes,
    intersections,
    coupling_fock,
    partner_owner,
    partner_slot,
):
    R, C = lax.axis_size("row"), lax.axis_size("col")
    G = R * C
    size = amplitudes.shape[0]
    pair_count = amplitudes.shape[2]
    occ_block = occ_energy.shape[0]
    pack = LANES // size
    depth = -(-pair_count // pack)
    depth += -depth % 4
    direct = G <= 16

    def packed_tiles(current):
        tiles = jnp.transpose(current.astype(jnp.bfloat16), (2, 0, 1))
        tiles = jnp.pad(tiles, ((0, pack * depth - pair_count), (0, 0), (0, 0)))
        parts = [tiles[t * depth : (t + 1) * depth] for t in range(pack)]
        spare = jnp.zeros((depth, size, LANES - pack * size), jnp.bfloat16)
        return jnp.concatenate(parts + [spare], axis=2)

    packed = packed_tiles(amplitudes)
    if direct:
        energy = jnp.pad(occ_energy[None, :], ((0, 7), (0, LANES - occ_block)))
        tiles, row_ints, col_ints, row_en, col_en = gather(packed, 1, orbital_ints, energy)
        row_energy = row_en[:, 0, :occ_block].reshape(-1)
        col_energy = col_en[:, 0, :occ_block].reshape(-1)
        row_ints = row_ints.reshape((-1,) + orbital_ints.shape[1:])
        col_ints = col_ints.reshape((-1,) + orbital_ints.shape[1:])
    else:
        tiles = lax.all_gather(packed, ("row", "col"), axis=0)
        row_ints = lax.all_gather(orbital_ints, "col", axis=0, tiled=True)
        col_ints = lax.all_gather(orbital_ints, "row", axis=0, tiled=True)
        row_energy = lax.all_gather(occ_energy, "col", axis=0, tiled=True)
        col_energy = lax.all_gather(occ_energy, "row", axis=0, tiled=True)
    seconds = col_ints.shape[0]
    exchange = jnp.einsum(
        "iax,jbx->ijab", row_ints, col_ints, preferred_element_type=jnp.float32
    ).reshape(-1, size, size)
    picks = pair_row * seconds + pair_col
    first_hot = (pair_row[:, None] == jnp.arange(row_energy.shape[0])[None, :])
    second_hot = (pair_col[:, None] == jnp.arange(seconds)[None, :])
    occupied = jnp.sum(jnp.where(first_hot, row_energy[None, :], 0.0), axis=1) + jnp.sum(
        jnp.where(second_hot, col_energy[None, :], 0.0), axis=1
    )
    denominator = virt_energy[:, None, :] + virt_energy[None, :, :] - occupied[None, None, :]
    owners = partner_owner[0].T.reshape(-1)
    slots = partner_slot[0].T.reshape(-1)
    turn = sum((slots >= t * depth).astype(jnp.int32) for t in range(1, pack))
    rows = owners * depth + slots - turn * depth
    shifts = turn * size
    fock = coupling_fock.reshape(-1)
    inter = jnp.transpose(intersections, (3, 2, 0, 1))
    spare = jnp.zeros(inter.shape[:3] + (LANES - pack * size,), inter.dtype)
    inter = jnp.concatenate([inter] * pack + [spare], axis=3)
    current = amplitudes
    residual = amplitudes
    base = exchange
    for step in range(ITERS):
        if step > 0:
            packed = packed_tiles(current)
            if direct:
                (tiles,) = gather(packed, 2)
            else:
                tiles = lax.all_gather(packed, ("row", "col"), axis=0)
        tiles = tiles.reshape(G * depth, size, LANES)
        part, *kept = couple(step == 0, rows, shifts, fock, picks, tiles, inter, base)
        change = fit_sum(jnp.transpose(part, (1, 2, 0)), 3).astype(jnp.float32)
        if step == 0:
            base = kept[0]
            total = change
        else:
            total = total + change
        residual = total + denominator * current
        current = current - residual / denominator
    return (current, residual)


def solution(mesh):
    placed = (
        P(("row", "col"), None, "fit"),
        P(("row", "col")),
        P(("row", "col")),
        P(("row", "col")),
        P(None, ("row", "col")),
        P(None, None, ("row", "col")),
        P(None, None, "fit", ("row", "col")),
        P("fit", ("row", "col")),
        P("fit", ("row", "col"), None),
        P("fit", ("row", "col"), None),
    )
    out = P(None, None, ("row", "col"))
    return jax.shard_map(
        on_device, mesh=mesh, in_specs=placed, out_specs=(out, out), check_vma=False
    )
```

time: 475 us -> 192 us (0.40)
  blocking collectives: 165 us -> 0 us
  Pallas kernels: 0 us -> 147 us
  local copies, waits for them, and re-layouts: 138 us -> 21.9 us
  waiting for transfers between devices: 63.5 us -> 0 us
  other arithmetic: 52.6 us -> 21.5 us
  matrix products: 26.6 us -> 0.44 us
  between operations: 15.5 us -> 0.8 us
  starting transfers between devices: 11.2 us -> 0 us
    pallas_call x0 -> x6, Pallas kernels: none -> 147 us  [the longest x2 68.5 us: gather(): pl.pallas_call(functools.partial(gather_kernel, (first, half - first), wi...]
    all_to_all x1 -> x0, blocking collectives: 78.5 us -> none  [on_device(): lax.all_to_all(outgoing, ('row', 'col'), split_axis=2, concat_axis=2, til...]
    unnamed x39 -> x21, local copies, waits for them, and re-layouts: 78.5 us -> 10.2 us
    psum x2 -> x0, waiting for transfers between devices: 60.9 us -> none  [the longest x1 30.7 us: on_device(): lax.psum(partial_kernel.astype(jnp.bfloat16), 'fit').astype(jnp.float32)]
    unnamed x2 -> x0, blocking collectives: 55.4 us -> none
    gather x8 -> x0, local copies, waits for them, and re-layouts: 47.4 us -> none  [the longest x2 22.1 us: on_device(): outgoing = jnp.take(sent_tiles, incoming, axis=2)]
    all_gather x2 -> x0, blocking collectives: 31.3 us -> none  [the longest x1 27 us: on_device(): lax.all_gather(orbital_ints, 'col', axis=0, tiled=True)]
    dot_general x3 -> x1, matrix products: 26.6 us -> 0.44 us  [on_device(): jnp.einsum('iax,jbx->ijab', row_ints, col_ints, preferred_element_type=jn...]
  transfers between devices with their start and end apart: 4 -> 0, of which waited for: 3 -> 0; matrix products, arithmetic and copies ran while one was open for 8% -> 0% of each run, Pallas kernels for 0% -> 0%
where the time goes in v1:
time: 192 us; the launch traced here: 191 us
  Pallas kernels  147 us (77%)
  local copies, waits for them, and re-layouts  21.9 us (11%)
  other arithmetic  21.5 us (11%)
    pallas_call x2, Pallas kernels, gather(): pl.pallas_call(functools.partial(gather_kernel, (first, half - first), wi...  68.5 us
    pallas_call x2, Pallas kernels, couple(): pl.pallas_call(functools.partial(couple_kernel, block, pair_count, first_...  50.4 us
    pallas_call x2, Pallas kernels, fit_sum(): pl.pallas_call(sum_kernel, out_shape=jax.ShapeDtypeStruct(part.shape, par...  27.7 us
    concatenate x1, other arithmetic, on_device(): inter = jnp.concatenate([inter] * pack + [spare], axis=3)  12.8 us
    unnamed x21, local copies, waits for them, and re-layouts  10.2 us
    pallas_call x2, local copies, waits for them, and re-layouts, couple(): pl.pallas_call(functools.partial(couple_kernel, block, pair_count, first_...  5.13 us

profile of v1, /device:TPU:1, one launch (start us, length us, event | category | flops | bytes accessed | tf_op | source)
XLA Modules:
  0.0 191.1 jit_solution(1036212630470127283)
XLA Ops:
  0.7 1.2 convert_element_type.35
  1.9 1.5 copy.42
  3.4 0.2 fusion.4
  3.7 1.2 maximum_maximum_fusion.1.refs_0_
  4.9 0.6 pad.12.refs_2_
  5.5 38.6 %gather_ints.1 = (bf16[8,44,40,128]{3,2,1,0:T(8,128)(2,1)}, bf16[4,2,40,640]{3,2,1,0:T(8,128)(2,1)}, bf16[2,2,40,640]{3,2,1,0:T(8,128)(2,1)}, f32[4,8,128]{2,1,0:T(8,128)}, f32[2,8,128]{2,1,0:T(8,128)}) custom-call(bf16[44,40,128]{2,1,0:T(8,128)(2,1)} %maximum_maximum_fusion.1.refs_0_, bf16[2,40,640]{2,1,0:T(8,128)(2,1)} %refs_1_.1, f32[8,128]{1,0:T(8,128)} %pad.12.refs_2_), custom_call_target="tpu_custom_call" | custom-call | tf_op jit(solution)/shard_map/gather_ints/pallas_call | solution.py:222
  44.2 0.7 slice_reduce_fusion
  44.9 0.1 broadcast_in_dim.43
  45.0 0.1 select_reduce_fusion
  45.1 0.7 slice_reduce_fusion.1
  45.8 0.1 broadcast_in_dim.46
  45.9 0.1 select_reduce_fusion.1
  46.0 0.6 multiply_bitcast_fusion
  46.6 0.5 multiply_add_fusion.pick_ref
  47.1 10.1 %copy.43 = bf16[40,40,4,128]{1,0,2,3:T(8,128)(2,1)} copy(bf16[40,40,4,128]{3,2,1,0:T(4,128)(2,1)} %param.16) | data formatting | bytes 3276800 | tf_op args[6]
  57.2 12.8 %maximum_maximum_fusion.inter = bf16[128,4,40,128]{3,2,1,0:T(8,128)(2,1)} fusion(bf16[128,4,40,40]{3,2,1,0:T(8,128)(2,1)} %bitcast.35, bf16[128]{0:T(256)(128)(2,1)S(1)} %pad.25.clone), kind=kLoop, calls=%fused_computation | loop fusion | flops 20971520 | bytes 6881536 | tf_op jit(solution)/shard_map/concatenate | solution.py:409
  70.0 0.4 convolution_bitcast_fusion
  70.5 1.1 copy.44
  71.5 25.3 %couple.2 = (bf16[128,40,40]{2,1,0:T(8,128)(2,1)}, f32[128,40,40]{2,1,0:T(8,128)}) custom-call(s32[512]{0:T(512)} %get-tuple-element.25.row_ref, s32[512]{0:T(512)} %get-tuple-element.24.shift_ref, f32[512]{0:T(512)} %bitcast.44, s32[128]{0:T(128)} %multiply_add_fusion.pick_ref, bf16[352,40,128]{2,1,0:T(8,128)(2,1)} %bitcast.38, ...), custom_call_target="tpu_custom_call" | custom-call | tf_op jit(solution)/shard_map/couple/pallas_call | solution.py:331
  96.8 2.6 %copy.45 = bf16[128,40,40]{0,2,1:T(8,128)(2,1)} copy(bf16[128,40,40]{2,1,0:T(8,128)(2,1)} %get-tuple-element.12) | data formatting | bytes 819200 | tf_op jit(solution)/shard_map/couple/pallas_call | solution.py:331
  99.4 13.9 %fit_sum.2 = bf16[40,40,128]{2,1,0:T(8,128)(2,1)} custom-call(bf16[40,40,128]{2,1,0:T(8,128)(2,1)} %bitcast.40), custom_call_target="tpu_custom_call" | custom-call | tf_op jit(solution)/shard_map/fit_sum/pallas_call | solution.py:274
  113.3 1.3 convert_bitcast_fusion
  114.6 0.3 fusion.5
  114.9 0.4 copy.48
  115.3 0.4 copy.47
  115.7 0.4 copy.46
  116.1 1.2 maximum_maximum_fusion.2.refs_0_
  117.3 29.8 %gather_tiles.1 = bf16[8,44,40,128]{3,2,1,0:T(8,128)(2,1)} custom-call(bf16[44,40,128]{2,1,0:T(8,128)(2,1)} %maximum_maximum_fusion.2.refs_0_), custom_call_target="tpu_custom_call" | custom-call | tf_op jit(solution)/shard_map/gather_tiles/pallas_call | solution.py:222
  147.2 25.1 %couple.3 = bf16[128,40,40]{2,1,0:T(8,128)(2,1)} custom-call(s32[512]{0:T(512)} %get-tuple-element.25.row_ref, s32[512]{0:T(512)} %get-tuple-element.24.shift_ref, f32[512]{0:T(512)} %bitcast.45, s32[128]{0:T(128)} %multiply_add_fusion.pick_ref, bf16[352,40,128]{2,1,0:T(8,128)(2,1)} %bitcast.36, bf16[128,4,40,128]{3,2,1,0:T(8,128)(2,1)} %maximum_maximum_fusion.inter, ...), custom_call_target="tpu_custom_call" | custom-call | tf_op jit(solution)/shard_map/couple/pallas_call | solution.py:331
  172.2 2.6 %copy.49 = bf16[128,40,40]{0,2,1:T(8,128)(2,1)} copy(bf16[128,40,40]{2,1,0:T(8,128)(2,1)} %couple.3) | data formatting | bytes 819200 | tf_op jit(solution)/shard_map/couple/pallas_call | solution.py:331
  174.8 13.7 %fit_sum.3 = bf16[40,40,128]{2,1,0:T(8,128)(2,1)} custom-call(bf16[40,40,128]{2,1,0:T(8,128)(2,1)} %bitcast.41), custom_call_target="tpu_custom_call" | custom-call | tf_op jit(solution)/shard_map/fit_sum/pallas_call | solution.py:274
  188.6 2.6 %divide_subtract_fusion = (f32[40,40,128]{2,1,0:T(8,128)}, f32[40,40,128]{2,1,0:T(8,128)}) fusion(f32[128]{0:T(128)S(1)} %add.66, f32[40,128]{1,0:T(8,128)S(1)} %copy-done.3, f32[40,40,128]{2,1,0:T(8,128)S(1)} %copy-done, bf16[40,40,128]{2,1,0:T(8,128)(2,1)S(1)} %copy-done.1, bf16[40,40,128]{2,1,0:T(8,128)(2,1)} %fit_sum.3), kind=kLoop, calls=%fused_computation.8 | loop fusion | flops 2662400 | bytes 3297792 | tf_op jit(solution)/shard_map/sub | solution.py:429
  (23 shorter events, 0.1 us)
Async XLA Ops:
  0.6 4.3 %copy-start.7 = (f32[2]{0:T(128)S(1)}, f32[2]{0:T(128)}, u32[]{:S(2)}) copy-start(f32[2]{0:T(128)} %param.11) | copy-start | bytes 28
  0.6 44.4 %copy-start.8 = (s32[128]{0:T(128)S(1)}, s32[128]{0:T(128)}, u32[]{:S(2)}) copy-start(s32[128]{0:T(128)} %param.12) | copy-start | bytes 1540
  0.7 45.2 %copy-start.9 = (s32[128]{0:T(128)S(1)}, s32[128]{0:T(128)}, u32[]{:S(2)}) copy-start(s32[128]{0:T(128)} %param.13) | copy-start | bytes 1540
  0.7 45.3 %copy-start.5 = (s32[1,128,4]{1,2,0:T(4,128)S(1)}, s32[1,128,4]{1,2,0:T(4,128)}, u32[]{:S(2)}) copy-start(s32[1,128,4]{1,2,0:T(4,128)} %param.19) | copy-start | bytes 6148
  0.7 45.3 %copy-start.6 = (s32[1,128,4]{1,2,0:T(4,128)S(1)}, s32[1,128,4]{1,2,0:T(4,128)}, u32[]{:S(2)}) copy-start(s32[1,128,4]{1,2,0:T(4,128)} %param.18) | copy-start | bytes 6148
  57.2 12.8 %copy-start.2 = (bf16[4,2,40,640]{3,2,1,0:T(8,128)(2,1)S(1)}, bf16[4,2,40,640]{3,2,1,0:T(8,128)(2,1)}, u32[]{:S(2)}) copy-start(bf16[4,2,40,640]{3,2,1,0:T(8,128)(2,1)} %get-tuple-element.11) | copy-start | bytes 1228804
  57.2 12.8 %copy-start.4 = (bf16[2,2,40,640]{3,2,1,0:T(8,128)(2,1)S(1)}, bf16[2,2,40,640]{3,2,1,0:T(8,128)(2,1)}, u32[]{:S(2)}) copy-start(bf16[2,2,40,640]{3,2,1,0:T(8,128)(2,1)} %get-tuple-element.10) | copy-start | bytes 614404
  71.5 41.8 %copy-start = (f32[40,40,128]{2,1,0:T(8,128)S(1)}, f32[40,40,128]{2,1,0:T(8,128)}, u32[]{:S(2)}) copy-start(f32[40,40,128]{2,1,0:T(8,128)} %param.15) | copy-start | bytes 2457604
  71.5 41.8 %copy-start.3 = (f32[40,128]{1,0:T(8,128)S(1)}, f32[40,128]{1,0:T(8,128)}, u32[]{:S(2)}) copy-start(f32[40,128]{1,0:T(8,128)} %param.14) | copy-start | bytes 61444
  147.2 41.4 %copy-start.1 = (bf16[40,40,128]{2,1,0:T(8,128)(2,1)S(1)}, bf16[40,40,128]{2,1,0:T(8,128)(2,1)}, u32[]{:S(2)}) copy-start(bf16[40,40,128]{2,1,0:T(8,128)(2,1)} %fit_sum.2) | copy-start | bytes 1228804

commit v2 on v1

--- a/solution.py
+++ b/solution.py
@@ -1,4 +1,5 @@
 import functools
+import math
 
 import jax
 import jax.numpy as jnp
@@ -70,12 +71,14 @@
     r, c, f = lax.axis_index("row"), lax.axis_index("col"), lax.axis_index("fit")
     partner = {"fit": f + 1 - 2 * lax.rem(f, 2)}
     half = sum(sizes)
+    count = len(sizes) // 2
+    lengthwise, crosswise = range(count), range(count, 2 * count)
     mine = lax.rem(f, 2) * half
     theirs = half - mine
     me = r * C + c
     greet(("row", "col", "fit"))
     out = Sender(send_sems)
-    offsets = (0, sizes[0])
+    offsets = [sum(sizes[:piece]) for piece in range(2 * count)]
 
     def place(piece, group, base=mine):
         return tiles.at[group, pl.ds(base + offsets[piece], sizes[piece])]
@@ -108,9 +111,10 @@
     def own_piece(piece):
         return own.at[pl.ds(mine + offsets[piece], sizes[piece])]
 
-    across(1, me, source=own_piece(1))
-    for step in (1, -1):
-        along(0, me, step, source=own_piece(0))
+    for long_piece, cross_piece in zip(lengthwise, crosswise):
+        across(cross_piece, me, source=own_piece(cross_piece))
+        for step in (1, -1):
+            along(long_piece, me, step, source=own_piece(long_piece))
     if with_ints:
         def int_wait(target, sem, when=None):
             copy = pltpu.make_async_remote_copy(
@@ -129,9 +133,10 @@
         for step in range(1, C):
             to = {"col": lax.rem(c + step, C)}
             out.send(energy, row_en.at[c], int_sems.at[2, c], to)
-    for step in (1, -1):
-        along(1, me, step, source=own_piece(1))
-    across(0, me, source=own_piece(0))
+    for long_piece, cross_piece in zip(lengthwise, crosswise):
+        for step in (1, -1):
+            along(cross_piece, me, step, source=own_piece(cross_piece))
+        across(long_piece, me, source=own_piece(long_piece))
     local = [pltpu.make_async_copy(own, tiles.at[me], local_sems.at[0])]
     if with_ints:
         local += [
@@ -142,29 +147,35 @@
         ]
     for copy in local:
         copy.start()
-    for other in range(1, R):
-        group = lax.rem(r + other, R) * C + c
-        await_copy(1, group, recv_sems.at[1, group])
-        for step in (1, -1):
-            along(1, group, step)
-        beside(1, group)
+    for piece in crosswise:
+        for other in range(1, R):
+            group = lax.rem(r + other, R) * C + c
+            await_copy(piece, group, recv_sems.at[piece, group])
+            for step in (1, -1):
+                along(piece, group, step)
+            beside(piece, group)
     for distance in range(1, C):
+        for long_piece, cross_piece in zip(lengthwise, crosswise):
+            for step in (1, -1):
+                source = c - step * distance
+                there = jnp.logical_and(source >= 0, source < C)
+                column = jnp.clip(source, 0, C - 1)
+                group = r * C + column
+                await_copy(long_piece, group, recv_sems.at[long_piece, group], when=there)
+                if distance < C - 1:
+                    along(long_piece, group, step, there)
+                across(long_piece, group, there)
+                beside(long_piece, group, there)
+                for other in range(R):
+                    group = lax.rem(r + other, R) * C + column
+                    await_copy(cross_piece, group, recv_sems.at[cross_piece, group], when=there)
+                    if distance < C - 1:
+                        along(cross_piece, group, step, there)
+                    beside(cross_piece, group, there)
         for step in (1, -1):
             source = c - step * distance
             there = jnp.logical_and(source >= 0, source < C)
             column = jnp.clip(source, 0, C - 1)
-            group = r * C + column
-            await_copy(0, group, recv_sems.at[0, group], when=there)
-            if distance < C - 1:
-                along(0, group, step, there)
-            across(0, group, there)
-            beside(0, group, there)
-            for other in range(R):
-                group = lax.rem(r + other, R) * C + column
-                await_copy(1, group, recv_sems.at[1, group], when=there)
-                if distance < C - 1:
-                    along(1, group, step, there)
-                beside(1, group, there)
             if with_ints:
                 int_wait(row_ints.at[column], int_sems.at[0, column], there)
                 if distance < C - 1:
@@ -176,8 +187,9 @@
     for other in range(1, R):
         for turn in range(C):
             group = lax.rem(r + other, R) * C + lax.rem(c + turn, C)
-            await_copy(0, group, recv_sems.at[0, group])
-            beside(0, group)
+            for piece in lengthwise:
+                await_copy(piece, group, recv_sems.at[piece, group])
+                beside(piece, group)
     if with_ints:
         for step in range(1, R):
             row = lax.rem(r + step, R)
@@ -188,7 +200,7 @@
             int_wait(row_en.at[column], int_sems.at[2, column])
     for step in range(1, R * C):
         group = lax.rem(me + step, R * C)
-        for piece in range(2):
+        for piece in range(2 * count):
             await_copy(piece, group, part_sems.at[piece, group], base=theirs)
     for copy in local:
         copy.wait()
@@ -201,6 +213,8 @@
     with_ints = ints is not None
     half = packed.shape[0] // 2
     first = (half * 3 + 4) // 5
+    count = max(1, min(3, half - first))
+    sizes = tuple(len(range(i, total, count)) for total in (first, half - first) for i in range(count))
     shapes = [jax.ShapeDtypeStruct((G,) + packed.shape, packed.dtype)]
     operands = [packed]
     if with_ints:
@@ -212,15 +226,15 @@
             jax.ShapeDtypeStruct((R,) + energy.shape, energy.dtype),
         ]
     scratch = [
-        pltpu.SemaphoreType.DMA((16 * R * C + 32,)),
-        pltpu.SemaphoreType.DMA((2, G)),
-        pltpu.SemaphoreType.DMA((2, G)),
+        pltpu.SemaphoreType.DMA((8 * len(sizes) * G + 32,)),
+        pltpu.SemaphoreType.DMA((len(sizes), G)),
+        pltpu.SemaphoreType.DMA((len(sizes), G)),
     ]
     if with_ints:
         scratch.append(pltpu.SemaphoreType.DMA((4, max(R, C))))
     scratch.append(pltpu.SemaphoreType.DMA((5,)))
     return pl.pallas_call(
-        functools.partial(gather_kernel, (first, half - first), with_ints),
+        functools.partial(gather_kernel, sizes, with_ints),
         out_shape=shapes,
         in_specs=[ANY] * len(operands),
         out_specs=[ANY] * len(shapes),
@@ -291,37 +305,38 @@
 
 def couple_kernel(block, pair_count, first_turn, row_ref, shift_ref, fock_ref, pick_ref, tiles, inter, base, out, *kept):
     links, size = inter.shape[1], inter.shape[2]
-    lane = lax.broadcasted_iota(jnp.int32, (1, LANES), 1)
     first = pl.program_id(0) * block
-
-    def pair(q, carry):
-        p = first + q
-        halves, sides = [], []
+    halves, results = [], []
+    for q in range(block):
         for k in range(links):
-            n = k * pair_count + p
-            side = inter[q, k]
-            half = jnp.dot(side[:, :size], tiles[row_ref[n]], preferred_element_type=jnp.float32)
-            shift = shift_ref[n]
-            chosen = jnp.logical_and(lane >= shift, lane < shift + size)
-            halves.append((half * jnp.where(chosen, fock_ref[n], 0.0)).astype(jnp.bfloat16))
-            sides.append(side)
-        coupling = lax.dot_general(
-            jnp.concatenate(halves, axis=1), jnp.concatenate(sides, axis=1),
-            (((1,), (1,)), ((), ())), preferred_element_type=jnp.float32,
+            n = k * pair_count + first + q
+            tile = pltpu.roll(tiles[row_ref[n]], shift_ref[n], 1)[:, :size]
+            halves.append(jnp.dot(inter[q, k], tile, preferred_element_type=jnp.float32))
+    for q in range(block):
+        for k in range(links):
+            scale = fock_ref[k * pair_count + first + q]
+            halves[q * links + k] = (halves[q * links + k] * scale).astype(jnp.bfloat16)
+    for q in range(block):
+        results.append(
+            sum(
+                lax.dot_general(
+                    halves[q * links + k], inter[q, k], (((1,), (1,)), ((), ())),
+                    preferred_element_type=jnp.float32,
+                )
+                for k in range(links)
+            )
         )
+    for q in range(block):
         if first_turn:
-            kept[0][q] = coupling
-            out[q] = (base[pick_ref[p]] - coupling).astype(out.dtype)
+            kept[0][q] = results[q]
+            out[q] = (base[pick_ref[first + q]] - results[q]).astype(out.dtype)
         else:
-            out[q] = (base[q] - coupling).astype(out.dtype)
-        return carry
-
-    lax.fori_loop(0, block, pair, 0, unroll=4)
+            out[q] = (base[q] - results[q]).astype(out.dtype)
 
 
 def couple(first_turn, rows, shifts, fock, picks, tiles, inter, base):
     pair_count, links, size, _ = inter.shape
-    block = 16
+    block = math.gcd(pair_count, 16)
     smem = pl.BlockSpec(memory_space=pltpu.SMEM)
     whole = lambda shape: pl.BlockSpec(shape, lambda i: (0, 0, 0), pipeline_mode=pl.Buffered(1))
     by_pair = pl.BlockSpec((block, size, size), lambda i: (i, 0, 0))
@@ -335,7 +350,7 @@
         in_specs=[
             smem, smem, smem, smem,
             whole(tiles.shape),
-            pl.BlockSpec((block, links, size, LANES), lambda i: (i, 0, 0, 0)),
+            pl.BlockSpec((block, links, size, size), lambda i: (i, 0, 0, 0)),
             whole(base.shape) if first_turn else by_pair,
         ],
         out_specs=[by_pair] * len(shapes),
@@ -402,11 +417,9 @@
     slots = partner_slot[0].T.reshape(-1)
     turn = sum((slots >= t * depth).astype(jnp.int32) for t in range(1, pack))
     rows = owners * depth + slots - turn * depth
-    shifts = turn * size
+    shifts = jnp.where(turn == 0, 0, LANES - turn * size)
     fock = coupling_fock.reshape(-1)
     inter = jnp.transpose(intersections, (3, 2, 0, 1))
-    spare = jnp.zeros(inter.shape[:3] + (LANES - pack * size,), inter.dtype)
-    inter = jnp.concatenate([inter] * pack + [spare], axis=3)
     current = amplitudes
     residual = amplitudes
     base = exchange

time: 192 us -> 160 us (0.83)
  Pallas kernels: 147 us -> 126 us
  other arithmetic: 21.5 us -> 10.1 us
    pallas_call x2, Pallas kernels: 50.4 us -> 24.5 us  [couple(): pl.pallas_call(functools.partial(couple_kernel, block, pair_count, first_...]
    concatenate x1 -> x0, other arithmetic: 12.8 us -> none  [on_device(): inter = jnp.concatenate([inter] * pack + [spare], axis=3)]
    pallas_call x2, Pallas kernels: 68.5 us -> 74.3 us  [gather(): pl.pallas_call(functools.partial(gather_kernel, sizes, with_ints), out_sh...]
    unnamed x21 -> x13, local copies, waits for them, and re-layouts: 10.2 us -> 8.05 us
where the time goes in v2:
time: 160 us; the launch traced here: 159 us
  Pallas kernels  126 us (79%)
  local copies, waits for them, and re-layouts  20.5 us (13%)
  other arithmetic  10.1 us (6%)
    pallas_call x2, Pallas kernels, gather(): pl.pallas_call(functools.partial(gather_kernel, sizes, with_ints), out_sh...  74.3 us
    pallas_call x2, Pallas kernels, fit_sum(): pl.pallas_call(sum_kernel, out_shape=jax.ShapeDtypeStruct(part.shape, par...  26.9 us
    pallas_call x2, Pallas kernels, couple(): pl.pallas_call(functools.partial(couple_kernel, block, pair_count, first_...  24.5 us
    unnamed x13, local copies, waits for them, and re-layouts  8.05 us
    pallas_call x2, local copies, waits for them, and re-layouts, couple(): pl.pallas_call(functools.partial(couple_kernel, block, pair_count, first_...  5.27 us

profile of v2, /device:TPU:1, one launch (start us, length us, event | category | flops | bytes accessed | tf_op | source)
XLA Modules:
  0.0 158.6 jit_solution(8576852648831581947)
XLA Ops:
  0.6 1.3 multiply_add_fusion.pick_ref
  1.9 0.1 pad.21.clone
  2.0 1.3 pad.12.refs_2_
  3.2 1.3 select_bitcast_fusion
  4.5 1.2 convert_element_type.35
  5.7 1.5 copy.42
  7.2 0.2 fusion.5
  7.5 1.2 maximum_maximum_fusion.refs_0_
  8.7 41.7 %gather_ints.1 = (bf16[8,44,40,128]{3,2,1,0:T(8,128)(2,1)}, bf16[4,2,40,640]{3,2,1,0:T(8,128)(2,1)}, bf16[2,2,40,640]{3,2,1,0:T(8,128)(2,1)}, f32[4,8,128]{2,1,0:T(8,128)}, f32[2,8,128]{2,1,0:T(8,128)}) custom-call(bf16[44,40,128]{2,1,0:T(8,128)(2,1)} %maximum_maximum_fusion.refs_0_, bf16[2,40,640]{2,1,0:T(8,128)(2,1)} %refs_1_.1, f32[8,128]{1,0:T(8,128)} %pad.12.refs_2_), custom_call_target="tpu_custom_call" | custom-call | tf_op jit(solution)/shard_map/gather_ints/pallas_call | solution.py:236
  50.4 0.7 slice_reduce_fusion.1
  51.1 0.1 broadcast_in_dim.44
  51.2 0.1 select_reduce_fusion.1
  51.3 0.7 slice_reduce_fusion
  52.0 0.1 broadcast_in_dim.41
  52.1 0.1 select_reduce_fusion
  52.2 1.6 convolution_bitcast_fusion
  53.8 1.1 copy.44
  54.9 8.0 %copy.43 = bf16[40,40,4,128]{1,0,2,3:T(8,128)(2,1)} copy(bf16[40,40,4,128]{3,2,1,0:T(4,128)(2,1)S(1)} %copy-done.2) | data formatting | bytes 3276800 | tf_op args[6]
  62.9 12.4 %couple.2 = (bf16[128,40,40]{2,1,0:T(8,128)(2,1)}, f32[128,40,40]{2,1,0:T(8,128)}) custom-call(s32[512]{0:T(512)} %get-tuple-element.25.row_ref, s32[512]{0:T(512)} %get-tuple-element.24.shift_ref, f32[512]{0:T(512)} %bitcast.45, s32[128]{0:T(128)} %multiply_add_fusion.pick_ref, bf16[352,40,128]{2,1,0:T(8,128)(2,1)} %bitcast.39, ...), custom_call_target="tpu_custom_call" | custom-call | tf_op jit(solution)/shard_map/couple/pallas_call | solution.py:346
  75.3 2.6 %copy.45 = bf16[128,40,40]{0,2,1:T(8,128)(2,1)} copy(bf16[128,40,40]{2,1,0:T(8,128)(2,1)} %get-tuple-element.12) | data formatting | bytes 819200 | tf_op jit(solution)/shard_map/couple/pallas_call | solution.py:346
  77.9 13.9 %fit_sum.2 = bf16[40,40,128]{2,1,0:T(8,128)(2,1)} custom-call(bf16[40,40,128]{2,1,0:T(8,128)(2,1)} %bitcast.41), custom_call_target="tpu_custom_call" | custom-call | tf_op jit(solution)/shard_map/fit_sum/pallas_call | solution.py:288
  91.9 1.2 convert_bitcast_fusion
  93.2 0.3 fusion.6
  93.4 0.4 copy.46
  93.8 0.4 copy.48
  94.2 0.4 copy.47
  94.6 1.2 maximum_maximum_fusion.1.refs_0_
  95.9 32.5 %gather_tiles.1 = bf16[8,44,40,128]{3,2,1,0:T(8,128)(2,1)} custom-call(bf16[44,40,128]{2,1,0:T(8,128)(2,1)} %maximum_maximum_fusion.1.refs_0_), custom_call_target="tpu_custom_call" | custom-call | tf_op jit(solution)/shard_map/gather_tiles/pallas_call | solution.py:236
  128.4 12.1 %couple.3 = bf16[128,40,40]{2,1,0:T(8,128)(2,1)} custom-call(s32[512]{0:T(512)} %get-tuple-element.25.row_ref, s32[512]{0:T(512)} %get-tuple-element.24.shift_ref, f32[512]{0:T(512)} %bitcast.46, s32[128]{0:T(128)} %multiply_add_fusion.pick_ref, bf16[352,40,128]{2,1,0:T(8,128)(2,1)} %bitcast.37, bf16[128,4,40,40]{3,2,1,0:T(8,128)(2,1)} %bitcast.36, ...), custom_call_target="tpu_custom_call" | custom-call | tf_op jit(solution)/shard_map/couple/pallas_call | solution.py:346
  140.5 2.6 %copy.49 = bf16[128,40,40]{0,2,1:T(8,128)(2,1)} copy(bf16[128,40,40]{2,1,0:T(8,128)(2,1)} %couple.3) | data formatting | bytes 819200 | tf_op jit(solution)/shard_map/couple/pallas_call | solution.py:346
  143.1 13.0 %fit_sum.3 = bf16[40,40,128]{2,1,0:T(8,128)(2,1)} custom-call(bf16[40,40,128]{2,1,0:T(8,128)(2,1)} %bitcast.42), custom_call_target="tpu_custom_call" | custom-call | tf_op jit(solution)/shard_map/fit_sum/pallas_call | solution.py:288
  156.1 2.5 %divide_subtract_fusion = (f32[40,40,128]{2,1,0:T(8,128)}, f32[40,40,128]{2,1,0:T(8,128)}) fusion(f32[128]{0:T(128)S(1)} %add.66, f32[40,128]{1,0:T(8,128)S(1)} %copy-done.3, f32[40,40,128]{2,1,0:T(8,128)S(1)} %copy-done, bf16[40,40,128]{2,1,0:T(8,128)(2,1)S(1)} %copy-done.1, bf16[40,40,128]{2,1,0:T(8,128)(2,1)} %fit_sum.3), kind=kLoop, calls=%fused_computation.7 | loop fusion | flops 2662400 | bytes 3297792 | tf_op jit(solution)/shard_map/sub | solution.py:442
  (14 shorter events, 0.0 us)
Async XLA Ops:
  7.4 43.8 %copy-start.4 = (s32[128]{0:T(128)S(1)}, s32[128]{0:T(128)}, u32[]{:S(2)}) copy-start(s32[128]{0:T(128)} %param.13) | copy-start | bytes 1540
  7.5 44.7 %copy-start.5 = (s32[128]{0:T(128)S(1)}, s32[128]{0:T(128)}, u32[]{:S(2)}) copy-start(s32[128]{0:T(128)} %param.12) | copy-start | bytes 1540
  8.7 46.2 %copy-start.2 = (bf16[40,40,4,128]{3,2,1,0:T(4,128)(2,1)S(1)}, bf16[40,40,4,128]{3,2,1,0:T(4,128)(2,1)}, u32[]{:S(2)}) copy-start(bf16[40,40,4,128]{3,2,1,0:T(4,128)(2,1)} %param.16) | copy-start | bytes 4915204
  75.3 16.6 %copy-start = (f32[40,40,128]{2,1,0:T(8,128)S(1)}, f32[40,40,128]{2,1,0:T(8,128)}, u32[]{:S(2)}) copy-start(f32[40,40,128]{2,1,0:T(8,128)} %param.15) | copy-start | bytes 2457604
  75.3 16.6 %copy-start.3 = (f32[40,128]{1,0:T(8,128)S(1)}, f32[40,128]{1,0:T(8,128)}, u32[]{:S(2)}) copy-start(f32[40,128]{1,0:T(8,128)} %param.14) | copy-start | bytes 61444
  140.5 15.6 %copy-start.1 = (bf16[40,40,128]{2,1,0:T(8,128)(2,1)S(1)}, bf16[40,40,128]{2,1,0:T(8,128)(2,1)}, u32[]{:S(2)}) copy-start(bf16[40,40,128]{2,1,0:T(8,128)(2,1)} %fit_sum.2) | copy-start | bytes 1228804

commit v3 on v2

--- a/solution.py
+++ b/solution.py
@@ -71,14 +71,14 @@
     r, c, f = lax.axis_index("row"), lax.axis_index("col"), lax.axis_index("fit")
     partner = {"fit": f + 1 - 2 * lax.rem(f, 2)}
     half = sum(sizes)
-    count = len(sizes) // 2
-    lengthwise, crosswise = range(count), range(count, 2 * count)
+    count = len(sizes)
+    pieces = range(count)
     mine = lax.rem(f, 2) * half
     theirs = half - mine
     me = r * C + c
     greet(("row", "col", "fit"))
     out = Sender(send_sems)
-    offsets = [sum(sizes[:piece]) for piece in range(2 * count)]
+    offsets = [sum(sizes[:piece]) for piece in pieces]
 
     def place(piece, group, base=mine):
         return tiles.at[group, pl.ds(base + offsets[piece], sizes[piece])]
@@ -111,10 +111,10 @@
     def own_piece(piece):
         return own.at[pl.ds(mine + offsets[piece], sizes[piece])]
 
-    for long_piece, cross_piece in zip(lengthwise, crosswise):
-        across(cross_piece, me, source=own_piece(cross_piece))
+    for piece in pieces:
         for step in (1, -1):
-            along(long_piece, me, step, source=own_piece(long_piece))
+            along(piece, me, step, source=own_piece(piece))
+        across(piece, me, source=own_piece(piece))
     if with_ints:
         def int_wait(target, sem, when=None):
             copy = pltpu.make_async_remote_copy(
@@ -133,10 +133,6 @@
         for step in range(1, C):
             to = {"col": lax.rem(c + step, C)}
             out.send(energy, row_en.at[c], int_sems.at[2, c], to)
-    for long_piece, cross_piece in zip(lengthwise, crosswise):
-        for step in (1, -1):
-            along(cross_piece, me, step, source=own_piece(cross_piece))
-        across(long_piece, me, source=own_piece(long_piece))
     local = [pltpu.make_async_copy(own, tiles.at[me], local_sems.at[0])]
     if with_ints:
         local += [
@@ -147,49 +143,54 @@
         ]
     for copy in local:
         copy.start()
-    for piece in crosswise:
+    events = []
+
+    def behind(step, distance):
+        source = c - step * distance
+        there = jnp.logical_and(source >= 0, source < C)
+        return jnp.clip(source, 0, C - 1), there
+
+    def arrival(piece, step, distance):
+        column, there = behind(step, distance)
+        group = r * C + column
+        await_copy(piece, group, recv_sems.at[piece, group], when=there)
+        if distance < C - 1:
+            along(piece, group, step, there)
+        across(piece, group, there)
+        beside(piece, group, there)
+
+    def crossed(piece, other, step, distance):
+        column, there = behind(step, distance)
+        group = lax.rem(r + other, R) * C + column
+        await_copy(piece, group, recv_sems.at[piece, group], when=there)
+        beside(piece, group, there)
+
+    def int_arrival(step, distance):
+        column, there = behind(step, distance)
+        int_wait(row_ints.at[column], int_sems.at[0, column], there)
+        if distance < C - 1:
+            inside = c + 1 < C if step > 0 else c > 0
+            out.send(
+                row_ints.at[column], row_ints.at[column], int_sems.at[0, column],
+                {"col": c + step}, both(there, inside),
+            )
+
+    for piece in pieces:
         for other in range(1, R):
-            group = lax.rem(r + other, R) * C + c
-            await_copy(piece, group, recv_sems.at[piece, group])
+            events.append((1.5, piece, functools.partial(crossed, piece, other, 1, 0)))
+        for distance in range(1, C):
             for step in (1, -1):
-                along(piece, group, step)
-            beside(piece, group)
-    for distance in range(1, C):
-        for long_piece, cross_piece in zip(lengthwise, crosswise):
+                events.append((distance, piece, functools.partial(arrival, piece, step, distance)))
+                for other in range(1, R):
+                    events.append((
+                        distance + 1.5, piece, functools.partial(crossed, piece, other, step, distance)
+                    ))
+    if with_ints:
+        for distance in range(1, C):
             for step in (1, -1):
-                source = c - step * distance
-                there = jnp.logical_and(source >= 0, source < C)
-                column = jnp.clip(source, 0, C - 1)
-                group = r * C + column
-                await_copy(long_piece, group, recv_sems.at[long_piece, group], when=there)
-                if distance < C - 1:
-                    along(long_piece, group, step, there)
-                across(long_piece, group, there)
-                beside(long_piece, group, there)
-                for other in range(R):
-                    group = lax.rem(r + other, R) * C + column
-                    await_copy(cross_piece, group, recv_sems.at[cross_piece, group], when=there)
-                    if distance < C - 1:
-                        along(cross_piece, group, step, there)
-                    beside(cross_piece, group, there)
-        for step in (1, -1):
-            source = c - step * distance
-            there = jnp.logical_and(source >= 0, source < C)
-            column = jnp.clip(source, 0, C - 1)
-            if with_ints:
-                int_wait(row_ints.at[column], int_sems.at[0, column], there)
-                if distance < C - 1:
-                    inside = c + 1 < C if step > 0 else c > 0
-                    out.send(
-                        row_ints.at[column], row_ints.at[column], int_sems.at[0, column],
-                        {"col": c + step}, both(there, inside),
-                    )
-    for other in range(1, R):
-        for turn in range(C):
-            group = lax.rem(r + other, R) * C + lax.rem(c + turn, C)
-            for piece in lengthwise:
-                await_copy(piece, group, recv_sems.at[piece, group])
-                beside(piece, group)
+                events.append((distance, count, functools.partial(int_arrival, step, distance)))
+    for _, _, event in sorted(events, key=lambda entry: entry[:2]):
+        event()
     if with_ints:
         for step in range(1, R):
             row = lax.rem(r + step, R)
@@ -200,7 +201,7 @@
             int_wait(row_en.at[column], int_sems.at[2, column])
     for step in range(1, R * C):
         group = lax.rem(me + step, R * C)
-        for piece in range(2 * count):
+        for piece in pieces:
             await_copy(piece, group, part_sems.at[piece, group], base=theirs)
     for copy in local:
         copy.wait()
@@ -212,9 +213,8 @@
     G = R * C
     with_ints = ints is not None
     half = packed.shape[0] // 2
-    first = (half * 3 + 4) // 5
-    count = max(1, min(3, half - first))
-    sizes = tuple(len(range(i, total, count)) for total in (first, half - first) for i in range(count))
+    count = min(2, half)
+    sizes = tuple(len(range(i, half, count)) for i in range(count))
     shapes = [jax.ShapeDtypeStruct((G,) + packed.shape, packed.dtype)]
     operands = [packed]
     if with_ints:

time: 160 us -> 145 us (0.906)
  Pallas kernels: 126 us -> 111 us
    pallas_call x2, Pallas kernels: 74.3 us -> 59.7 us  [gather(): pl.pallas_call(functools.partial(gather_kernel, sizes, with_ints), out_sh...]
where the time goes in v3:
time: 145 us; the launch traced here: 144 us
  Pallas kernels  111 us (77%)
  local copies, waits for them, and re-layouts  20.5 us (14%)
  other arithmetic  10.1 us (7%)
  matrix products  1.55 us (1%)
    pallas_call x2, Pallas kernels, gather(): pl.pallas_call(functools.partial(gather_kernel, sizes, with_ints), out_sh...  59.7 us
    pallas_call x2, Pallas kernels, fit_sum(): pl.pallas_call(sum_kernel, out_shape=jax.ShapeDtypeStruct(part.shape, par...  27.2 us
    pallas_call x2, Pallas kernels, couple(): pl.pallas_call(functools.partial(couple_kernel, block, pair_count, first_...  24.5 us
    unnamed x13, local copies, waits for them, and re-layouts  8.05 us
    pallas_call x2, local copies, waits for them, and re-layouts, couple(): pl.pallas_call(functools.partial(couple_kernel, block, pair_count, first_...  5.27 us

profile of v3, /device:TPU:1, one launch (start us, length us, event | category | flops | bytes accessed | tf_op | source)
XLA Modules:
  0.0 144.4 jit_solution(12168496123584848132)
XLA Ops:
  0.6 1.3 multiply_add_fusion.pick_ref
  1.9 0.1 pad.21.clone
  2.0 1.3 pad.12.refs_2_
  3.2 1.3 select_bitcast_fusion
  4.5 1.2 convert_element_type.35
  5.7 1.5 %copy.42 = bf16[40,40,128]{1,0,2:T(8,128)(2,1)S(1)} copy(bf16[40,40,128]{2,1,0:T(8,128)(2,1)S(1)} %convert_element_type.35) | data formatting | bytes 819200 | tf_op jit(solution)/shard_map/convert_element_type | solution.py:385
  7.2 0.2 fusion.5
  7.5 1.2 maximum_maximum_fusion.refs_0_
  8.7 34.3 %gather_ints.1 = (bf16[8,44,40,128]{3,2,1,0:T(8,128)(2,1)}, bf16[4,2,40,640]{3,2,1,0:T(8,128)(2,1)}, bf16[2,2,40,640]{3,2,1,0:T(8,128)(2,1)}, f32[4,8,128]{2,1,0:T(8,128)}, f32[2,8,128]{2,1,0:T(8,128)}) custom-call(bf16[44,40,128]{2,1,0:T(8,128)(2,1)} %maximum_maximum_fusion.refs_0_, bf16[2,40,640]{2,1,0:T(8,128)(2,1)} %refs_1_.1, f32[8,128]{1,0:T(8,128)} %pad.12.refs_2_), custom_call_target="tpu_custom_call" | custom-call | tf_op jit(solution)/shard_map/gather_ints/pallas_call | solution.py:236
  43.0 0.7 slice_reduce_fusion.1
  43.7 0.1 broadcast_in_dim.44
  43.8 0.1 select_reduce_fusion.1
  43.9 0.7 slice_reduce_fusion
  44.6 0.1 broadcast_in_dim.41
  44.7 0.1 select_reduce_fusion
  44.8 1.6 %convolution_bitcast_fusion = f32[8,4,40,40]{2,3,0,1:T(8,128)S(1)} fusion(bf16[4,40,640,1]{2,1,3,0:T(8,128)(2,1)} %bitcast.44, bf16[8,40,640,1]{2,1,0,3:T(8,128)(2,1)} %bitcast.43), kind=kOutput, calls=%fused_computation.1 | convolution fusion | flops 65536000 | bytes 819200 | tf_op jit(solution)/shard_map/iax,jbx->ijab/dot_general | solution.py:406
  46.4 1.1 copy.44
  47.5 8.0 %copy.43 = bf16[40,40,4,128]{1,0,2,3:T(8,128)(2,1)} copy(bf16[40,40,4,128]{3,2,1,0:T(4,128)(2,1)S(1)} %copy-done.2) | data formatting | bytes 3276800 | tf_op args[6]
  55.5 12.4 %couple.2 = (bf16[128,40,40]{2,1,0:T(8,128)(2,1)}, f32[128,40,40]{2,1,0:T(8,128)}) custom-call(s32[512]{0:T(512)} %get-tuple-element.25.row_ref, s32[512]{0:T(512)} %get-tuple-element.24.shift_ref, f32[512]{0:T(512)} %bitcast.45, s32[128]{0:T(128)} %multiply_add_fusion.pick_ref, bf16[352,40,128]{2,1,0:T(8,128)(2,1)} %bitcast.39, ...), custom_call_target="tpu_custom_call" | custom-call | tf_op jit(solution)/shard_map/couple/pallas_call | solution.py:346
  67.9 2.6 %copy.45 = bf16[128,40,40]{0,2,1:T(8,128)(2,1)} copy(bf16[128,40,40]{2,1,0:T(8,128)(2,1)} %get-tuple-element.12) | data formatting | bytes 819200 | tf_op jit(solution)/shard_map/couple/pallas_call | solution.py:346
  70.5 13.9 %fit_sum.2 = bf16[40,40,128]{2,1,0:T(8,128)(2,1)} custom-call(bf16[40,40,128]{2,1,0:T(8,128)(2,1)} %bitcast.41), custom_call_target="tpu_custom_call" | custom-call | tf_op jit(solution)/shard_map/fit_sum/pallas_call | solution.py:288
  84.5 1.2 convert_bitcast_fusion
  85.7 0.3 fusion.6
  86.0 0.4 copy.46
  86.4 0.4 copy.48
  86.8 0.4 copy.47
  87.2 1.2 maximum_maximum_fusion.1.refs_0_
  88.4 25.4 %gather_tiles.1 = bf16[8,44,40,128]{3,2,1,0:T(8,128)(2,1)} custom-call(bf16[44,40,128]{2,1,0:T(8,128)(2,1)} %maximum_maximum_fusion.1.refs_0_), custom_call_target="tpu_custom_call" | custom-call | tf_op jit(solution)/shard_map/gather_tiles/pallas_call | solution.py:236
  113.9 12.1 %couple.3 = bf16[128,40,40]{2,1,0:T(8,128)(2,1)} custom-call(s32[512]{0:T(512)} %get-tuple-element.25.row_ref, s32[512]{0:T(512)} %get-tuple-element.24.shift_ref, f32[512]{0:T(512)} %bitcast.46, s32[128]{0:T(128)} %multiply_add_fusion.pick_ref, bf16[352,40,128]{2,1,0:T(8,128)(2,1)} %bitcast.37, bf16[128,4,40,40]{3,2,1,0:T(8,128)(2,1)} %bitcast.36, ...), custom_call_target="tpu_custom_call" | custom-call | tf_op jit(solution)/shard_map/couple/pallas_call | solution.py:346
  126.0 2.6 %copy.49 = bf16[128,40,40]{0,2,1:T(8,128)(2,1)} copy(bf16[128,40,40]{2,1,0:T(8,128)(2,1)} %couple.3) | data formatting | bytes 819200 | tf_op jit(solution)/shard_map/couple/pallas_call | solution.py:346
  128.6 13.3 %fit_sum.3 = bf16[40,40,128]{2,1,0:T(8,128)(2,1)} custom-call(bf16[40,40,128]{2,1,0:T(8,128)(2,1)} %bitcast.42), custom_call_target="tpu_custom_call" | custom-call | tf_op jit(solution)/shard_map/fit_sum/pallas_call | solution.py:288
  141.9 2.5 %divide_subtract_fusion = (f32[40,40,128]{2,1,0:T(8,128)}, f32[40,40,128]{2,1,0:T(8,128)}) fusion(f32[128]{0:T(128)S(1)} %add.66, f32[40,128]{1,0:T(8,128)S(1)} %copy-done.3, f32[40,40,128]{2,1,0:T(8,128)S(1)} %copy-done, bf16[40,40,128]{2,1,0:T(8,128)(2,1)S(1)} %copy-done.1, bf16[40,40,128]{2,1,0:T(8,128)(2,1)} %fit_sum.3), kind=kLoop, calls=%fused_computation.7 | loop fusion | flops 2662400 | bytes 3297792 | tf_op jit(solution)/shard_map/sub | solution.py:442
  (14 shorter events, 0.0 us)
Async XLA Ops:
  7.4 36.4 %copy-start.4 = (s32[128]{0:T(128)S(1)}, s32[128]{0:T(128)}, u32[]{:S(2)}) copy-start(s32[128]{0:T(128)} %param.13) | copy-start | bytes 1540
  7.5 37.3 %copy-start.5 = (s32[128]{0:T(128)S(1)}, s32[128]{0:T(128)}, u32[]{:S(2)}) copy-start(s32[128]{0:T(128)} %param.12) | copy-start | bytes 1540
  8.7 38.8 %copy-start.2 = (bf16[40,40,4,128]{3,2,1,0:T(4,128)(2,1)S(1)}, bf16[40,40,4,128]{3,2,1,0:T(4,128)(2,1)}, u32[]{:S(2)}) copy-start(bf16[40,40,4,128]{3,2,1,0:T(4,128)(2,1)} %param.16) | copy-start | bytes 4915204
  67.9 16.6 %copy-start = (f32[40,40,128]{2,1,0:T(8,128)S(1)}, f32[40,40,128]{2,1,0:T(8,128)}, u32[]{:S(2)}) copy-start(f32[40,40,128]{2,1,0:T(8,128)} %param.15) | copy-start | bytes 2457604
  67.9 16.6 %copy-start.3 = (f32[40,128]{1,0:T(8,128)S(1)}, f32[40,128]{1,0:T(8,128)}, u32[]{:S(2)}) copy-start(f32[40,128]{1,0:T(8,128)} %param.14) | copy-start | bytes 61444
  126.0 15.9 %copy-start.1 = (bf16[40,40,128]{2,1,0:T(8,128)(2,1)S(1)}, bf16[40,40,128]{2,1,0:T(8,128)(2,1)}, u32[]{:S(2)}) copy-start(bf16[40,40,128]{2,1,0:T(8,128)(2,1)} %fit_sum.2) | copy-start | bytes 1228804

commit v4 on v3

--- a/solution.py
+++ b/solution.py
@@ -303,7 +303,10 @@
     )(part)
 
 
-def couple_kernel(block, pair_count, first_turn, row_ref, shift_ref, fock_ref, pick_ref, tiles, inter, base, out, *kept):
+def couple_kernel(
+    block, pair_count, first_turn, seconds, row_ref, shift_ref, fock_ref, first_ref, second_ref, tiles, inter, base,
+    out, *kept
+):
     links, size = inter.shape[1], inter.shape[2]
     first = pl.program_id(0) * block
     halves, results = [], []
@@ -329,14 +332,15 @@
     for q in range(block):
         if first_turn:
             kept[0][q] = results[q]
-            out[q] = (base[pick_ref[first + q]] - results[q]).astype(out.dtype)
+            pick = first_ref[first + q] * seconds + second_ref[first + q]
+            out[q] = (base[pick] - results[q]).astype(out.dtype)
         else:
             out[q] = (base[q] - results[q]).astype(out.dtype)
 
 
-def couple(first_turn, rows, shifts, fock, picks, tiles, inter, base):
+def couple(first_turn, seconds, rows, shifts, fock, firsts, others, tiles, inter, base):
     pair_count, links, size, _ = inter.shape
-    block = math.gcd(pair_count, 16)
+    block = math.gcd(pair_count, 32)
     smem = pl.BlockSpec(memory_space=pltpu.SMEM)
     whole = lambda shape: pl.BlockSpec(shape, lambda i: (0, 0, 0), pipeline_mode=pl.Buffered(1))
     by_pair = pl.BlockSpec((block, size, size), lambda i: (i, 0, 0))
@@ -344,11 +348,11 @@
     if first_turn:
         shapes.append(jax.ShapeDtypeStruct((pair_count, size, size), jnp.float32))
     return pl.pallas_call(
-        functools.partial(couple_kernel, block, pair_count, first_turn),
+        functools.partial(couple_kernel, block, pair_count, first_turn, seconds),
         grid=(pair_count // block,),
         out_shape=shapes,
         in_specs=[
-            smem, smem, smem, smem,
+            smem, smem, smem, smem, smem,
             whole(tiles.shape),
             pl.BlockSpec((block, links, size, size), lambda i: (i, 0, 0, 0)),
             whole(base.shape) if first_turn else by_pair,
@@ -356,7 +360,7 @@
         out_specs=[by_pair] * len(shapes),
         name="couple",
         compiler_params=pltpu.CompilerParams(vmem_limit_bytes=VMEM_LIMIT),
-    )(rows, shifts, fock, picks, tiles, inter, base)
+    )(rows, shifts, fock, firsts, others, tiles, inter, base)
 
 
 def on_device(
@@ -406,7 +410,6 @@
     exchange = jnp.einsum(
         "iax,jbx->ijab", row_ints, col_ints, preferred_element_type=jnp.float32
     ).reshape(-1, size, size)
-    picks = pair_row * seconds + pair_col
     first_hot = (pair_row[:, None] == jnp.arange(row_energy.shape[0])[None, :])
     second_hot = (pair_col[:, None] == jnp.arange(seconds)[None, :])
     occupied = jnp.sum(jnp.where(first_hot, row_energy[None, :], 0.0), axis=1) + jnp.sum(
@@ -431,7 +434,9 @@
             else:
                 tiles = lax.all_gather(packed, ("row", "col"), axis=0)
         tiles = tiles.reshape(G * depth, size, LANES)
-        part, *kept = couple(step == 0, rows, shifts, fock, picks, tiles, inter, base)
+        part, *kept = couple(
+            step == 0, seconds, rows, shifts, fock, pair_row, pair_col, tiles, inter, base
+        )
         change = fit_sum(jnp.transpose(part, (1, 2, 0)), 3).astype(jnp.float32)
         if step == 0:
             base = kept[0]

time: 145 us -> 141 us (0.972)
  Pallas kernels: 111 us -> 109 us
    pallas_call x2, Pallas kernels: 24.5 us -> 22.1 us  [couple(): pl.pallas_call(functools.partial(couple_kernel, block, pair_count, first_...]
where the time goes in v4:
time: 141 us
  Pallas kernels  109 us (77%)
  local copies, waits for them, and re-layouts  20.5 us (15%)
  other arithmetic  8.89 us (6%)
  matrix products  1.55 us (1%)
    pallas_call x2, Pallas kernels, gather(): pl.pallas_call(functools.partial(gather_kernel, sizes, with_ints), out_sh...  59.7 us
    pallas_call x2, Pallas kernels, fit_sum(): pl.pallas_call(sum_kernel, out_shape=jax.ShapeDtypeStruct(part.shape, par...  27.2 us
    pallas_call x2, Pallas kernels, couple(): pl.pallas_call(functools.partial(couple_kernel, block, pair_count, first_...  22.1 us
    unnamed x13, local copies, waits for them, and re-layouts  8.05 us
    pallas_call x2, local copies, waits for them, and re-layouts, couple(): pl.pallas_call(functools.partial(couple_kernel, block, pair_count, first_...  5.27 us

profile of v4, /device:TPU:1, one launch (start us, length us, event | category | flops | bytes accessed | tf_op | source)
XLA Modules:
  0.0 140.8 jit_solution(3355966275308393743)
XLA Ops:
  0.6 0.1 pad.21.clone
  0.7 1.3 pad.12.refs_2_
  2.0 1.3 select_bitcast_fusion
  3.3 1.2 convert_element_type.35
  4.5 1.5 %copy.42 = bf16[40,40,128]{1,0,2:T(8,128)(2,1)S(1)} copy(bf16[40,40,128]{2,1,0:T(8,128)(2,1)S(1)} %convert_element_type.35) | data formatting | bytes 819200 | tf_op jit(solution)/shard_map/convert_element_type | solution.py:389
  5.9 0.2 fusion.5
  6.2 0.0 copy-start.4
  6.2 1.2 maximum_maximum_fusion.refs_0_
  7.4 34.3 %gather_ints.1 = (bf16[8,44,40,128]{3,2,1,0:T(8,128)(2,1)}, bf16[4,2,40,640]{3,2,1,0:T(8,128)(2,1)}, bf16[2,2,40,640]{3,2,1,0:T(8,128)(2,1)}, f32[4,8,128]{2,1,0:T(8,128)}, f32[2,8,128]{2,1,0:T(8,128)}) custom-call(bf16[44,40,128]{2,1,0:T(8,128)(2,1)} %maximum_maximum_fusion.refs_0_, bf16[2,40,640]{2,1,0:T(8,128)(2,1)} %refs_1_.1, f32[8,128]{1,0:T(8,128)} %pad.12.refs_2_), custom_call_target="tpu_custom_call" | custom-call | tf_op jit(solution)/shard_map/gather_ints/pallas_call | solution.py:236
  41.8 0.7 slice_reduce_fusion.1
  42.5 0.1 broadcast_in_dim.44
  42.6 0.1 select_reduce_fusion.1
  42.6 0.7 slice_reduce_fusion
  43.4 0.1 broadcast_in_dim.41
  43.5 0.1 select_reduce_fusion
  43.6 1.6 %convolution_bitcast_fusion = f32[8,4,40,40]{2,3,0,1:T(8,128)S(1)} fusion(bf16[4,40,640,1]{2,1,3,0:T(8,128)(2,1)} %bitcast.44, bf16[8,40,640,1]{2,1,0,3:T(8,128)(2,1)} %bitcast.43), kind=kOutput, calls=%fused_computation.1 | convolution fusion | flops 65536000 | bytes 819200 | tf_op jit(solution)/shard_map/iax,jbx->ijab/dot_general | solution.py:410
  45.1 1.1 copy.44
  46.2 8.0 %copy.43 = bf16[40,40,4,128]{1,0,2,3:T(8,128)(2,1)} copy(bf16[40,40,4,128]{3,2,1,0:T(4,128)(2,1)S(1)} %copy-done.2) | data formatting | bytes 3276800 | tf_op args[6]
  54.2 11.1 %couple.2 = (bf16[128,40,40]{2,1,0:T(8,128)(2,1)}, f32[128,40,40]{2,1,0:T(8,128)}) custom-call(s32[512]{0:T(512)} %get-tuple-element.25.row_ref, s32[512]{0:T(512)} %get-tuple-element.24.shift_ref, f32[512]{0:T(512)} %bitcast.45, s32[128]{0:T(128)} %first_ref.3, s32[128]{0:T(128)} %second_ref.3, bf16[352,40,128]{2,1,0:T(8,128)(2,1)} %bitcast.39, ...), custom_call_target="tpu_custom_call" | custom-call | tf_op jit(solution)/shard_map/couple/pallas_call | solution.py:350
  65.3 2.6 %copy.45 = bf16[128,40,40]{0,2,1:T(8,128)(2,1)} copy(bf16[128,40,40]{2,1,0:T(8,128)(2,1)} %get-tuple-element.12) | data formatting | bytes 819200 | tf_op jit(solution)/shard_map/couple/pallas_call | solution.py:350
  68.0 13.9 %fit_sum.2 = bf16[40,40,128]{2,1,0:T(8,128)(2,1)} custom-call(bf16[40,40,128]{2,1,0:T(8,128)(2,1)} %bitcast.41), custom_call_target="tpu_custom_call" | custom-call | tf_op jit(solution)/shard_map/fit_sum/pallas_call | solution.py:288
  81.9 1.2 convert_bitcast_fusion
  83.2 0.3 fusion.6
  83.5 0.4 copy.46
  83.9 0.4 copy.48
  84.3 0.4 copy.47
  84.7 1.2 maximum_maximum_fusion.1.refs_0_
  85.9 25.4 %gather_tiles.1 = bf16[8,44,40,128]{3,2,1,0:T(8,128)(2,1)} custom-call(bf16[44,40,128]{2,1,0:T(8,128)(2,1)} %maximum_maximum_fusion.1.refs_0_), custom_call_target="tpu_custom_call" | custom-call | tf_op jit(solution)/shard_map/gather_tiles/pallas_call | solution.py:236
  111.3 11.0 %couple.3 = bf16[128,40,40]{2,1,0:T(8,128)(2,1)} custom-call(s32[512]{0:T(512)} %get-tuple-element.25.row_ref, s32[512]{0:T(512)} %get-tuple-element.24.shift_ref, f32[512]{0:T(512)} %bitcast.46, s32[128]{0:T(128)} %first_ref.3, s32[128]{0:T(128)} %second_ref.3, bf16[352,40,128]{2,1,0:T(8,128)(2,1)} %bitcast.37, bf16[128,4,40,40]{3,2,1,0:T(8,128)(2,1)} %bitcast.36, ...), custom_call_target="tpu_custom_call" | custom-call | tf_op jit(solution)/shard_map/couple/pallas_call | solution.py:350
  122.3 2.6 %copy.49 = bf16[128,40,40]{0,2,1:T(8,128)(2,1)} copy(bf16[128,40,40]{2,1,0:T(8,128)(2,1)} %couple.3) | data formatting | bytes 819200 | tf_op jit(solution)/shard_map/couple/pallas_call | solution.py:350
  124.9 13.3 %fit_sum.3 = bf16[40,40,128]{2,1,0:T(8,128)(2,1)} custom-call(bf16[40,40,128]{2,1,0:T(8,128)(2,1)} %bitcast.42), custom_call_target="tpu_custom_call" | custom-call | tf_op jit(solution)/shard_map/fit_sum/pallas_call | solution.py:288
  138.2 2.5 %divide_subtract_fusion = (f32[40,40,128]{2,1,0:T(8,128)}, f32[40,40,128]{2,1,0:T(8,128)}) fusion(f32[128]{0:T(128)S(1)} %add.62, f32[40,128]{1,0:T(8,128)S(1)} %copy-done.3, f32[40,40,128]{2,1,0:T(8,128)S(1)} %copy-done, bf16[40,40,128]{2,1,0:T(8,128)(2,1)S(1)} %copy-done.1, bf16[40,40,128]{2,1,0:T(8,128)(2,1)} %fit_sum.3), kind=kLoop, calls=%fused_computation.7 | loop fusion | flops 2662400 | bytes 3297792 | tf_op jit(solution)/shard_map/sub | solution.py:447
  (13 shorter events, 0.0 us)
Async XLA Ops:
  6.2 36.4 %copy-start.5 = (s32[128]{0:T(128)S(1)}, s32[128]{0:T(128)}, u32[]{:S(2)}) copy-start(s32[128]{0:T(128)} %second_ref.3) | copy-start | bytes 1540
  6.2 37.3 %copy-start.4 = (s32[128]{0:T(128)S(1)}, s32[128]{0:T(128)}, u32[]{:S(2)}) copy-start(s32[128]{0:T(128)} %first_ref.3) | copy-start | bytes 1540
  7.4 38.8 %copy-start.2 = (bf16[40,40,4,128]{3,2,1,0:T(4,128)(2,1)S(1)}, bf16[40,40,4,128]{3,2,1,0:T(4,128)(2,1)}, u32[]{:S(2)}) copy-start(bf16[40,40,4,128]{3,2,1,0:T(4,128)(2,1)} %param.16) | copy-start | bytes 4915204
  65.3 16.6 %copy-start = (f32[40,40,128]{2,1,0:T(8,128)S(1)}, f32[40,40,128]{2,1,0:T(8,128)}, u32[]{:S(2)}) copy-start(f32[40,40,128]{2,1,0:T(8,128)} %param.15) | copy-start | bytes 2457604
  65.3 16.6 %copy-start.3 = (f32[40,128]{1,0:T(8,128)S(1)}, f32[40,128]{1,0:T(8,128)}, u32[]{:S(2)}) copy-start(f32[40,128]{1,0:T(8,128)} %param.14) | copy-start | bytes 61444
  122.3 15.9 %copy-start.1 = (bf16[40,40,128]{2,1,0:T(8,128)(2,1)S(1)}, bf16[40,40,128]{2,1,0:T(8,128)(2,1)}, u32[]{:S(2)}) copy-start(bf16[40,40,128]{2,1,0:T(8,128)(2,1)} %fit_sum.2) | copy-start | bytes 1228804
